TPU v7x, 512 devices: a whole 4x4x16 slice. The times are simulated.
512 devices in a mesh: wide: 128 (over z, y, core), narrow: 4 (over x).
Axes of the slice: x: 4, y: 4, z: 16, core: 2. Of those that a mesh axis runs over, the one named last changes fastest.
Arguments:
- trace_guess: float32 [128, 4, 16, 128, 128], P('wide', 'narrow'), may hold values from -6 to 6
- trace_rhs: float32 [128, 4, 16, 128, 128], P('wide', 'narrow'), may hold values from -6 to 6
- block_inverse: bfloat16 [128, 4, 16, 128, 128], P('wide', 'narrow')
- coupling: bfloat16 [128, 4, 16, 2, 128, 128], P('wide', 'narrow'), may hold values from -0.1875 to 0.1875
- block_neighbours: int32 [128, 4, 16, 2], P('wide', 'narrow'), may hold values from 0 to 23
- block_send: int32 [128, 4, 4, 2], P('wide', 'narrow'), may hold values from 0 to 15
- cell_faces: int32 [128, 4, 6, 2048], P('wide', 'narrow'), may hold values from 0 to 3071
- face_coeff: float32 [128, 4, 6, 2048], P('wide', 'narrow'), may hold values from 0.2 to 2
- cell_source: float32 [128, 4, 2048], P('wide', 'narrow'), may hold values from -6 to 6
- cell_neighbours: int32 [128, 4, 6, 2048], P('wide', 'narrow'), may hold values from 0 to 3071, as said below
- upwind_flags: int32 [128, 4, 6, 2048], P('wide', 'narrow'), may hold values 0 or 1
- cell_send: int32 [128, 4, 4, 256], P('wide', 'narrow'), may hold values from 0 to 2047
- saturation: float32 [128, 4, 4, 2048], P('wide', 'narrow'), may hold values from -3 to 3
- step_ratio: float32 [128, 4, 2048], P('wide', 'narrow'), may hold values from 0.05 to 0.2
Outputs:
- traces: float32 [128, 4, 16, 128, 128], P('wide', 'narrow')
- saturation_next: float32 [128, 4, 4, 2048], P('wide', 'narrow')
Inputs may be any that keep to these rules, and one draw needn't show every extreme that they name: `cell_neighbours`: faces 0 to 3 (f) index either an own cell (below 2048) or a cell of their own side's range, 2048 + f * 256 to 2048 + (f + 1) * 256 - 1; faces 4 and 5 index own cells only.
All inputs are finite; a program needn't handle non-finite values. No bound on the sum of `upwind_flags` on one device may be relied on, other than what follows from the above.
Results may differ from a plain program's by a relative error of at most 0.003.
Values may be sent and summed in bfloat16 or wider, within the bound.
A program may use at most 64 MiB of HBM per device.

v0:
```python
import jax
import jax.numpy as jnp
from jax import lax
from jax.sharding import PartitionSpec as P

lane_width = 128


def with_halo(block, sides, width):
    for axis, dim in sides:
        count = lax.axis_size(axis)
        forward = [(i, i + 1) for i in range(count - 1)]
        backward = [(target, source) for source, target in forward]
        low = lax.ppermute(
            lax.slice_in_dim(block, block.shape[dim] - width, None, axis=dim), axis, forward
        )
        high = lax.ppermute(lax.slice_in_dim(block, 0, width, axis=dim), axis, backward)
        block = jnp.concatenate([low, block, high], axis=dim)
    return block


def pick_blocks(table, index):
    count = table.shape[0]
    flat = table.reshape(count, -1)
    chooser = index.reshape(-1, 1) == lax.broadcasted_iota(jnp.int32, (1, count), 1)
    chosen = jnp.dot(chooser.astype(jnp.bfloat16), flat, preferred_element_type=jnp.float32).astype(
        jnp.bfloat16
    )
    return chosen.reshape(index.shape + table.shape[1:])


def lookup(values, index):
    modes, length = values.shape
    padded_len = -(-length // lane_width) * lane_width
    groups = padded_len // lane_width
    table = values.reshape(modes, groups, lane_width)
    high_part = index // lane_width
    low_part = index - high_part * lane_width
    high_hot = (high_part[:, None] == lax.broadcasted_iota(jnp.int32, (1, groups), 1)).astype(
        jnp.float32
    )
    low_hot = (low_part[:, None] == lax.broadcasted_iota(jnp.int32, (1, lane_width), 1)).astype(
        jnp.float32
    )
    lanes = jnp.einsum(
        "nh,mhl->mnl",
        high_hot,
        table,
        precision=lax.Precision.HIGHEST,
        preferred_element_type=jnp.float32,
    )
    return jnp.sum(lanes * low_hot[None], -1)


def trade_blocks(pieces):
    along_wide = with_halo(pieces[0:2], (("wide", 0),), 1)
    along_narrow = with_halo(pieces[2:4], (("narrow", 0),), 1)
    return jnp.concatenate(
        [along_wide[0:1], along_wide[3:4], along_narrow[0:1], along_narrow[3:4]], 0
    )


def trade_cells(pieces):
    along_wide = with_halo(pieces[0:2], (("wide", 0),), 1)
    along_narrow = with_halo(pieces[2:4], (("narrow", 0),), 1)
    return jnp.concatenate(
        [along_wide[0:1], along_wide[3:4], along_narrow[0:1], along_narrow[3:4]], 0
    )


def smooth(extended, inverse, couple, links, rhs):
    near = pick_blocks(extended, links)
    coupled = jnp.einsum("bkij,bkrj->bri", couple, near, preferred_element_type=jnp.float32)
    resid = (rhs - coupled).astype(jnp.bfloat16)
    return jnp.einsum("bij,brj->bri", inverse, resid, preferred_element_type=jnp.float32)


def per_device(
    trace_guess,
    trace_rhs,
    block_inverse,
    coupling,
    block_neighbours,
    block_send,
    cell_faces,
    face_coeff,
    cell_source,
    cell_neighbours,
    upwind_flags,
    cell_send,
    saturation,
    step_ratio,
):
    guess = trace_guess[0, 0]
    rhs = trace_rhs[0, 0]
    inverse = block_inverse[0, 0]
    couple = coupling[0, 0]
    links = block_neighbours[0, 0]
    sends = block_send[0, 0].reshape(-1)
    blocks, columns, faces = guess.shape
    current = guess.astype(jnp.bfloat16)
    outgoing = pick_blocks(current, sends)
    fresh = guess
    for sweep in range(2):
        arrived = trade_blocks(outgoing.reshape((4, -1) + outgoing.shape[1:]))
        extended = jnp.concatenate([current, arrived.reshape((-1,) + current.shape[1:])], 0)
        fresh = smooth(extended, inverse, couple, links, rhs)
        current = fresh.astype(jnp.bfloat16)
        edge = pick_blocks(current, sends)
        outgoing = edge if sweep == 0 else edge[:, 0:1, :]
    arrived = trade_blocks(outgoing.reshape(4, -1, 1, faces))
    face_values = (
        jnp.concatenate([current[:, 0, :], arrived.reshape(-1, faces)], 0)
        .reshape(1, -1)
        .astype(jnp.float32)
    )
    face_index = cell_faces[0, 0]
    face_trace = jnp.concatenate([lookup(face_values, face_index[face]) for face in range(6)], 0)
    coeff = face_coeff[0, 0]
    total = jnp.sum(coeff, 0)
    pressure = (cell_source[0, 0] + jnp.sum(coeff * face_trace, 0)) / total
    flux = coeff * (pressure[None, :] - face_trace)
    modes_now = saturation[0, 0]
    outbound = cell_send[0, 0]
    neighbours = cell_neighbours[0, 0]
    flags = upwind_flags[0, 0]
    ratio = step_ratio[0, 0]
    sent_modes = lookup(modes_now, outbound.reshape(-1)).reshape(4, 4, -1)
    flows = []
    pieces = jnp.transpose(sent_modes, (1, 0, 2))
    arrived_cells = trade_cells(pieces)
    ext_modes = jnp.concatenate(
        [modes_now, jnp.transpose(arrived_cells, (1, 0, 2)).reshape(4, -1)], 1
    )
    for face in range(6):
        axis_mode = face // 2 + 1
        sign = -1.0 if face % 2 == 0 else 1.0
        picked_modes = lookup(ext_modes, neighbours[face])
        across = picked_modes[0] - sign * picked_modes[axis_mode]
        own = modes_now[0] + sign * modes_now[axis_mode]
        flows.append(flux[face] * jnp.where(flags[face] == 1, own, across))
    flow = jnp.stack(flows, 0)
    result = [modes_now[0] - ratio * jnp.sum(flow, 0)]
    for axis_mode in range(1, 4):
        low, high = (2 * axis_mode - 2, 2 * axis_mode - 1)
        volume = 0.5 * (flux[high] - flux[low]) * modes_now[0]
        result.append(modes_now[axis_mode] + 3.0 * ratio * (volume - (flow[high] - flow[low])))
    return (fresh[None, None], jnp.stack(result, 0)[None, None])


def solution(mesh):
    placed = (
        P("wide", "narrow", None, None, None),
        P("wide", "narrow", None, None, None),
        P("wide", "narrow", None, None, None),
        P("wide", "narrow", None, None, None, None),
        P("wide", "narrow", None, None),
        P("wide", "narrow", None, None),
        P("wide", "narrow", None, None),
        P("wide", "narrow", None, None),
        P("wide", "narrow", None),
        P("wide", "narrow", None, None),
        P("wide", "narrow", None, None),
        P("wide", "narrow", None, None),
        P("wide", "narrow", None, None),
        P("wide", "narrow", None),
    )
    return jax.shard_map(
        per_device,
        mesh=mesh,
        in_specs=placed,
        out_specs=(P("wide", "narrow", None, None, None), P("wide", "narrow", None, None)),
        check_vma=False,
    )
```

profile of v0, /device:TPU:253, one launch (start us, length us, event | category | flops | bytes accessed | tf_op | source)
XLA Modules:
  0.0 110.2 jit_solution(16963377620763719435)
XLA Ops:
  0.6 0.9 copy.22
  1.6 1.3 %convert_element_type.115 = bf16[1,1,16,128,128]{4,3,2,1,0:T(8,128)(2,1)S(1)} convert(f32[1,1,16,128,128]{4,3,2,1,0:T(8,128)} %param.14) | non-fusion elementwise | flops 262144 | bytes 1572864 | tf_op jit(solution)/shard_map/convert_element_type | solution.py:101
  3.6 5.0 %collective-permute-start = (bf16[1,2,128,128]{3,2,1,0:T(8,128)(2,1)S(1)}, bf16[1,2,128,128]{3,2,1,0:T(8,128)(2,1)S(1)}, u32[]{:S(2)}, u32[]{:S(2)}) collective-permute-start(bf16[1,2,128,128]{3,2,1,0:T(8,128)(2,1)S(1)} %copy.108), channel_id=1, source_target_pairs={{0,4},{4,8},{8,12},{12,16},{16,20},{20,24},{24,28},{28,32},{32,36}... | collective-permute-start | bytes 196616 | tf_op jit(solution)/shard_map/ppermute | solution.py:14
  8.7 1.1 multiply_reduce_fusion
  10.4 1.9 %collective-permute-start.12 = (f32[1,4,256]{2,0,1:T(1,128)}, f32[1,4,256]{2,0,1:T(1,128)}, u32[]{:S(2)}, u32[]{:S(2)}) collective-permute-start(f32[1,4,256]{2,0,1:T(1,128)} %get-tuple-element.36), channel_id=1, source_target_pairs={{0,4},{4,8},{8,12},{12,16},{16,20},{20,24},{24,28},{28,32},{32,36}... | collective-permute-start | bytes 12296 | tf_op jit(solution)/shard_map/ppermute | solution.py:14
  12.3 2.4 %collective-permute-start.13 = (f32[1,4,256]{2,0,1:T(1,128)}, f32[1,4,256]{2,0,1:T(1,128)}, u32[]{:S(2)}, u32[]{:S(2)}) collective-permute-start(f32[1,4,256]{2,0,1:T(1,128)} %get-tuple-element.39), channel_id=1, source_target_pairs={{4,0},{8,4},{12,8},{16,12},{20,16},{24,20},{28,24},{32,28},{36,32}... | collective-permute-start | bytes 12296 | tf_op jit(solution)/shard_map/ppermute | solution.py:17
  14.8 2.8 %collective-permute-start.14 = (f32[1,4,256]{2,0,1:T(1,128)}, f32[1,4,256]{2,0,1:T(1,128)}, u32[]{:S(2)}, u32[]{:S(2)}) collective-permute-start(f32[1,4,256]{2,0,1:T(1,128)} %get-tuple-element.38), channel_id=1, source_target_pairs={{0,1},{1,2},{2,3},{4,5},{5,6},{6,7},{8,9},{9,10},{10,11},{12,13},{... | collective-permute-start | bytes 12296 | tf_op jit(solution)/shard_map/ppermute | solution.py:14
  17.6 2.4 %collective-permute-start.15 = (f32[1,4,256]{2,0,1:T(1,128)}, f32[1,4,256]{2,0,1:T(1,128)}, u32[]{:S(2)}, u32[]{:S(2)}) collective-permute-start(f32[1,4,256]{2,0,1:T(1,128)} %get-tuple-element.37), channel_id=1, source_target_pairs={{1,0},{2,1},{3,2},{5,4},{6,5},{7,6},{9,8},{10,9},{11,10},{13,12},{... | collective-permute-start | bytes 12296 | tf_op jit(solution)/shard_map/ppermute | solution.py:17
  20.1 0.6 multiply_subtract_fusion.6
  20.7 0.6 multiply_subtract_fusion.7
  24.5 1.1 fusion.36
  26.2 1.1 %fusion.35 = f32[2048,128]{0,1:T(8,128)} fusion(s32[2048]{0:T(1024)S(1)} %get-tuple-element.45), kind=kLoop, calls=%fused_computation.72 | loop fusion | flops 524288 | bytes 1056768 | tf_op jit(solution)/shard_map/convert_element_type | solution.py:42
  27.9 1.1 fusion.34
  29.6 1.1 fusion.33
  31.3 1.1 fusion.32
  32.4 0.6 multiply_subtract_fusion.11
  33.4 0.8 copy.21
  34.3 2.5 %collective-permute-start.1 = (bf16[1,2,128,128]{3,2,1,0:T(8,128)(2,1)S(1)}, bf16[1,2,128,128]{3,2,1,0:T(8,128)(2,1)S(1)}, u32[]{:S(2)}, u32[]{:S(2)}) collective-permute-start(bf16[1,2,128,128]{3,2,1,0:T(8,128)(2,1)S(1)} %copy.107), channel_id=1, source_target_pairs={{4,0},{8,4},{12,8},{16,12},{20,16},{24,20},{28,24},{32,28},{36,32}... | collective-permute-start | bytes 196616 | tf_op jit(solution)/shard_map/ppermute | solution.py:17
  36.8 3.4 %collective-permute-start.2 = (bf16[1,2,128,128]{3,2,1,0:T(8,128)(2,1)S(1)}, bf16[1,2,128,128]{3,2,1,0:T(8,128)(2,1)S(1)}, u32[]{:S(2)}, u32[]{:S(2)}) collective-permute-start(bf16[1,2,128,128]{3,2,1,0:T(8,128)(2,1)S(1)} %copy.106), channel_id=1, source_target_pairs={{0,1},{1,2},{2,3},{4,5},{5,6},{6,7},{8,9},{9,10},{10,11},{12,13},{... | collective-permute-start | bytes 196616 | tf_op jit(solution)/shard_map/ppermute | solution.py:14
  40.2 2.1 %collective-permute-start.3 = (bf16[1,2,128,128]{3,2,1,0:T(8,128)(2,1)S(1)}, bf16[1,2,128,128]{3,2,1,0:T(8,128)(2,1)S(1)}, u32[]{:S(2)}, u32[]{:S(2)}) collective-permute-start(bf16[1,2,128,128]{3,2,1,0:T(8,128)(2,1)S(1)} %copy.105), channel_id=1, source_target_pairs={{1,0},{2,1},{3,2},{5,4},{6,5},{7,6},{9,8},{10,9},{11,10},{13,12},{... | collective-permute-start | bytes 196616 | tf_op jit(solution)/shard_map/ppermute | solution.py:17
  42.4 0.7 maximum_bitcast_fusion.2
  43.1 3.4 %fusion = f32[4,2048]{1,0:T(4,128)} fusion(f32[2048,128]{0,1:T(8,128)S(1)} %fusion.37, s32[2048]{0:T(1024)} %get-tuple-element.40, f32[1,4,24,128]{3,1,2,0:T(4,128)S(1)} %maximum_bitcast_fusion), kind=kOutput, calls=%fused_computation.6 | convolution fusion | flops 304128000 | bytes 1138688 | tf_op jit(solution)/shard_map/nh,mhl->mnl/dot_general | solution.py:45
  46.5 2.7 %fusion.1 = f32[4,2048]{1,0:T(4,128)} fusion(f32[2048,128]{0,1:T(8,128)S(1)} %copy-done.4, s32[2048]{0:T(1024)S(1)} %copy-done.33, f32[1,4,24,128]{3,1,2,0:T(4,128)S(1)} %maximum_bitcast_fusion), kind=kOutput, calls=%fused_computation.8 | convolution fusion | flops 304128000 | bytes 1138688 | tf_op jit(solution)/shard_map/nh,mhl->mnl/dot_general | solution.py:45
  49.2 2.7 %fusion.2 = f32[4,2048]{1,0:T(4,128)} fusion(f32[2048,128]{0,1:T(8,128)S(1)} %copy-done.5, s32[2048]{0:T(1024)S(1)} %copy-done.34, f32[1,4,24,128]{3,1,2,0:T(4,128)S(1)} %maximum_bitcast_fusion), kind=kOutput, calls=%fused_computation.10 | convolution fusion | flops 304128000 | bytes 1138688 | tf_op jit(solution)/shard_map/nh,mhl->mnl/dot_general | solution.py:45
  51.9 2.7 %fusion.3 = f32[4,2048]{1,0:T(4,128)} fusion(f32[2048,128]{0,1:T(8,128)S(1)} %copy-done.6, s32[2048]{0:T(1024)S(1)} %copy-done.35, f32[1,4,24,128]{3,1,2,0:T(4,128)S(1)} %maximum_bitcast_fusion), kind=kOutput, calls=%fused_computation.12 | convolution fusion | flops 304128000 | bytes 1138688 | tf_op jit(solution)/shard_map/nh,mhl->mnl/dot_general | solution.py:45
  55.4 1.2 %copy.33 = bf16[4,8,128,128]{3,2,1,0:T(8,128)(2,1)} copy(bf16[4,8,128,128]{3,1,2,0:T(8,128)(2,1)S(1)} %fusion.12) | data formatting | bytes 2097152
  57.1 2.0 %convolution_convert_fusion.5 = bf16[16,128,128]{2,1,0:T(8,128)(2,1)S(1)} fusion(bf16[16,2,128,128]{3,2,1,0:T(8,128)(2,1)} %bitcast.413, bf16[1,1,16,2,128,128]{5,4,3,2,1,0:T(8,128)(2,1)S(1)} %copy-done, f32[1,1,16,128,128]{4,3,2,1,0:T(8,128)S(1)} %copy-done.1, bf16[1,1,16,128,128]{4,3,2,1,0:T(8,128)(2,1)S(1)} %copy-done.2), kind=kOutput, calls=%fused_computation.38 | convolution fusion | flops 202113024 | bytes 4194304 | tf_op jit(solution)/shard_map/bij,brj->bri/dot_general | solution.py:75
  59.7 7.0 %collective-permute-start.4 = (bf16[1,2,128,128]{3,2,1,0:T(8,128)(2,1)S(1)}, bf16[1,2,128,128]{3,2,1,0:T(8,128)(2,1)S(1)}, u32[]{:S(2)}, u32[]{:S(2)}) collective-permute-start(bf16[1,2,128,128]{3,2,1,0:T(8,128)(2,1)S(1)} %copy.104), channel_id=1, source_target_pairs={{0,4},{4,8},{8,12},{12,16},{16,20},{20,24},{24,28},{28,32},{32,36}... | collective-permute-start | bytes 196616 | tf_op jit(solution)/shard_map/ppermute | solution.py:14
  66.8 1.9 %collective-permute-start.5 = (bf16[1,2,128,128]{3,2,1,0:T(8,128)(2,1)S(1)}, bf16[1,2,128,128]{3,2,1,0:T(8,128)(2,1)S(1)}, u32[]{:S(2)}, u32[]{:S(2)}) collective-permute-start(bf16[1,2,128,128]{3,2,1,0:T(8,128)(2,1)S(1)} %copy.103), channel_id=1, source_target_pairs={{4,0},{8,4},{12,8},{16,12},{20,16},{24,20},{28,24},{32,28},{36,32}... | collective-permute-start | bytes 196616 | tf_op jit(solution)/shard_map/ppermute | solution.py:17
  68.7 3.4 %collective-permute-start.6 = (bf16[1,2,128,128]{3,2,1,0:T(8,128)(2,1)S(1)}, bf16[1,2,128,128]{3,2,1,0:T(8,128)(2,1)S(1)}, u32[]{:S(2)}, u32[]{:S(2)}) collective-permute-start(bf16[1,2,128,128]{3,2,1,0:T(8,128)(2,1)S(1)} %copy.102), channel_id=1, source_target_pairs={{0,1},{1,2},{2,3},{4,5},{5,6},{6,7},{8,9},{9,10},{10,11},{12,13},{... | collective-permute-start | bytes 196616 | tf_op jit(solution)/shard_map/ppermute | solution.py:14
  72.1 2.1 %collective-permute-start.7 = (bf16[1,2,128,128]{3,2,1,0:T(8,128)(2,1)S(1)}, bf16[1,2,128,128]{3,2,1,0:T(8,128)(2,1)S(1)}, u32[]{:S(2)}, u32[]{:S(2)}) collective-permute-start(bf16[1,2,128,128]{3,2,1,0:T(8,128)(2,1)S(1)} %copy.101), channel_id=1, source_target_pairs={{1,0},{2,1},{3,2},{5,4},{6,5},{7,6},{9,8},{10,9},{11,10},{13,12},{... | collective-permute-start | bytes 196616 | tf_op jit(solution)/shard_map/ppermute | solution.py:17
  74.3 2.1 %fusion.4 = f32[4,2048]{1,0:T(4,128)S(1)} fusion(f32[2048,128]{0,1:T(8,128)S(1)} %copy-done.3, s32[2048]{0:T(1024)S(1)} %copy-done.32, f32[1,4,24,128]{3,1,2,0:T(4,128)S(1)} %copy-done.13), kind=kOutput, calls=%fused_computation.14 | convolution fusion | flops 304128000 | bytes 1138688 | tf_op jit(solution)/shard_map/nh,mhl->mnl/dot_general | solution.py:45
  78.1 2.9 %fusion.152 = (bf16[16,128,128]{2,1,0:T(8,128)(2,1)}, f32[16,128,128]{2,1,0:T(8,128)}) fusion(bf16[1,1,16,128,128]{4,3,2,1,0:T(8,128)(2,1)} %param.16, bf16[16,2,128,128]{3,2,1,0:T(8,128)(2,1)S(1)} %bitcast.412, bf16[1,1,16,2,128,128]{5,4,3,2,1,0:T(8,128)(2,1)S(1)} %copy-done, f32[1,1,16,128,128]{4,3,2,1,0:T(8,128)S(1)} %copy-done.1), kind=kOutput, calls=%fused_computation.325 | convolution fusion | flops 202113024 | bytes 5242880 | tf_op jit(solution)/shard_map/bij,brj->bri/dot_general | solution.py:75
  81.1 1.4 %fusion.25 = bf16[8,128,128]{2,0,1:T(8,128)(2,1)S(1)} fusion(bf16[2,8,128,128]{3,2,1,0:T(8,128)(2,1)} %bitcast.414, s32[8]{0:T(128)S(1)} %copy-done.38), kind=kOutput, calls=%fused_computation.46 | convolution fusion | flops 4325504 | bytes 786464 | tf_op jit(solution)/shard_map/dot_general | solution.py:26
  82.5 3.0 %collective-permute-start.10 = (bf16[1,2,1,128]{3,1,2,0:T(2,128)(2,1)S(1)}, bf16[1,2,1,128]{3,1,2,0:T(2,128)(2,1)S(1)}, u32[]{:S(2)}, u32[]{:S(2)}) collective-permute-start(bf16[1,2,1,128]{3,1,2,0:T(2,128)(2,1)S(1)} %get-tuple-element.11), channel_id=1, source_target_pairs={{0,1},{1,2},{2,3},{4,5},{5,6},{6,7},{8,9},{9,10},{10,11},{12,13},{... | collective-permute-start | bytes 1544 | tf_op jit(solution)/shard_map/ppermute | solution.py:14
  85.6 2.2 %collective-permute-start.11 = (bf16[1,2,1,128]{3,1,2,0:T(2,128)(2,1)S(1)}, bf16[1,2,1,128]{3,1,2,0:T(2,128)(2,1)S(1)}, u32[]{:S(2)}, u32[]{:S(2)}) collective-permute-start(bf16[1,2,1,128]{3,1,2,0:T(2,128)(2,1)S(1)} %get-tuple-element.10), channel_id=1, source_target_pairs={{1,0},{2,1},{3,2},{5,4},{6,5},{7,6},{9,8},{10,9},{11,10},{13,12},{... | collective-permute-start | bytes 1544 | tf_op jit(solution)/shard_map/ppermute | solution.py:17
  87.8 9.0 %collective-permute-start.8 = (bf16[1,2,1,128]{3,1,2,0:T(2,128)(2,1)S(1)}, bf16[1,2,1,128]{3,1,2,0:T(2,128)(2,1)S(1)}, u32[]{:S(2)}, u32[]{:S(2)}) collective-permute-start(bf16[1,2,1,128]{3,1,2,0:T(2,128)(2,1)S(1)} %get-tuple-element.9), channel_id=1, source_target_pairs={{0,4},{4,8},{8,12},{12,16},{16,20},{20,24},{24,28},{28,32},{32,36}... | collective-permute-start | bytes 1544 | tf_op jit(solution)/shard_map/ppermute | solution.py:14
  96.8 1.9 %collective-permute-start.9 = (bf16[1,2,1,128]{3,1,2,0:T(2,128)(2,1)S(1)}, bf16[1,2,1,128]{3,1,2,0:T(2,128)(2,1)S(1)}, u32[]{:S(2)}, u32[]{:S(2)}) collective-permute-start(bf16[1,2,1,128]{3,1,2,0:T(2,128)(2,1)S(1)} %get-tuple-element.12), channel_id=1, source_target_pairs={{4,0},{8,4},{12,8},{16,12},{20,16},{24,20},{28,24},{32,28},{36,32}... | collective-permute-start | bytes 1544 | tf_op jit(solution)/shard_map/ppermute | solution.py:17
  98.7 3.2 %fusion.5 = f32[4,2048]{1,0:T(4,128)S(1)} fusion(f32[2048,128]{0,1:T(8,128)} %fusion.32, s32[2048]{0:T(1024)S(1)} %copy-done.31, f32[1,4,24,128]{3,1,2,0:T(4,128)S(1)} %copy-done.13), kind=kOutput, calls=%fused_computation.16 | convolution fusion | flops 304128000 | bytes 1138688 | tf_op jit(solution)/shard_map/nh,mhl->mnl/dot_general | solution.py:45
  102.0 0.8 slice.360
  102.8 2.2 %collective-permute-done.9 = bf16[1,2,1,128]{3,1,2,0:T(2,128)(2,1)S(1)} collective-permute-done((bf16[1,2,1,128]{3,1,2,0:T(2,128)(2,1)S(1)}, bf16[1,2,1,128]{3,1,2,0:T(2,128)(2,1)S(1)}, u32[]{:S(2)}, u32[]{:S(2)}) %collective-permute-start.9) | collective-permute-done | bytes 544 | tf_op jit(solution)/shard_map/ppermute | solution.py:17
  105.0 0.6 fusion.18
  105.7 0.6 fusion.19
  106.4 0.6 fusion.20
  107.1 0.6 fusion.21
  107.7 0.6 fusion.22
  108.4 0.6 fusion.23
  109.6 0.7 maximum_bitcast_fusion.1
  (151 shorter events, 11.6 us)
Async XLA Ops:
  0.6 55.9 %copy-start = (bf16[1,1,16,2,128,128]{5,4,3,2,1,0:T(8,128)(2,1)S(1)}, bf16[1,1,16,2,128,128]{5,4,3,2,1,0:T(8,128)(2,1)}, u32[]{:S(2)}) copy-start(bf16[1,1,16,2,128,128]{5,4,3,2,1,0:T(8,128)(2,1)} %param.17) | copy-start | bytes 3145732
  1.6 1.4 %copy-start.37 = (s32[8]{0:T(128)}, s32[8]{0:T(128)S(1)}, u32[]{:S(2)}) copy-start(s32[8]{0:T(128)S(1)} %eq.547) | copy-start | bytes 100
  2.9 5.7 %copy-start.41 = (s32[1,1,4,256]{3,2,1,0:T(4,128)S(1)}, s32[1,1,4,256]{3,2,1,0:T(4,128)}, u32[]{:S(2)}) copy-start(s32[1,1,4,256]{3,2,1,0:T(4,128)} %param.25) | copy-start | bytes 12292
  2.9 5.8 %copy-start.8 = (f32[1,1,4,2048]{3,2,1,0:T(4,128)S(1)}, f32[1,1,4,2048]{3,2,1,0:T(4,128)}, u32[]{:S(2)}) copy-start(f32[1,1,4,2048]{3,2,1,0:T(4,128)} %param.26) | copy-start | bytes 98308
  3.3 16.7 %copy-start.10 = (s32[1,1,6,2048]{3,1,2,0:T(1,128)S(1)}, s32[1,1,6,2048]{3,1,2,0:T(1,128)}, u32[]{:S(2)}) copy-start(s32[1,1,6,2048]{3,1,2,0:T(1,128)} %param.20) | copy-start | bytes 147460
  3.6 19.6 %copy-start.11 = (s32[1,1,6,2048]{3,1,2,0:T(1,128)S(1)}, s32[1,1,6,2048]{3,1,2,0:T(1,128)}, u32[]{:S(2)}) copy-start(s32[1,1,6,2048]{3,1,2,0:T(1,128)} %param.23) | copy-start | bytes 147460
  3.6 51.0 %collective-permute-start = (bf16[1,2,128,128]{3,2,1,0:T(8,128)(2,1)S(1)}, bf16[1,2,128,128]{3,2,1,0:T(8,128)(2,1)S(1)}, u32[]{:S(2)}, u32[]{:S(2)}) collective-permute-start(bf16[1,2,128,128]{3,2,1,0:T(8,128)(2,1)S(1)} %copy.108), channel_id=1, source_target_pairs={{0,4},{4,8},{8,12},{12,16},{16,20},{20,24},{24,28},{28,32},{32,36}... | collective-permute-start | bytes 196616 | tf_op jit(solution)/shard_map/ppermute | solution.py:14
  10.4 23.9 %collective-permute-start.12 = (f32[1,4,256]{2,0,1:T(1,128)}, f32[1,4,256]{2,0,1:T(1,128)}, u32[]{:S(2)}, u32[]{:S(2)}) collective-permute-start(f32[1,4,256]{2,0,1:T(1,128)} %get-tuple-element.36), channel_id=1, source_target_pairs={{0,4},{4,8},{8,12},{12,16},{16,20},{20,24},{24,28},{28,32},{32,36}... | collective-permute-start | bytes 12296 | tf_op jit(solution)/shard_map/ppermute | solution.py:14
  12.3 24.5 %collective-permute-start.13 = (f32[1,4,256]{2,0,1:T(1,128)}, f32[1,4,256]{2,0,1:T(1,128)}, u32[]{:S(2)}, u32[]{:S(2)}) collective-permute-start(f32[1,4,256]{2,0,1:T(1,128)} %get-tuple-element.39), channel_id=1, source_target_pairs={{4,0},{8,4},{12,8},{16,12},{20,16},{24,20},{28,24},{32,28},{36,32}... | collective-permute-start | bytes 12296 | tf_op jit(solution)/shard_map/ppermute | solution.py:17
  14.8 25.5 %collective-permute-start.14 = (f32[1,4,256]{2,0,1:T(1,128)}, f32[1,4,256]{2,0,1:T(1,128)}, u32[]{:S(2)}, u32[]{:S(2)}) collective-permute-start(f32[1,4,256]{2,0,1:T(1,128)} %get-tuple-element.38), channel_id=1, source_target_pairs={{0,1},{1,2},{2,3},{4,5},{5,6},{6,7},{8,9},{9,10},{10,11},{12,13},{... | collective-permute-start | bytes 12296 | tf_op jit(solution)/shard_map/ppermute | solution.py:14
  17.6 24.8 %collective-permute-start.15 = (f32[1,4,256]{2,0,1:T(1,128)}, f32[1,4,256]{2,0,1:T(1,128)}, u32[]{:S(2)}, u32[]{:S(2)}) collective-permute-start(f32[1,4,256]{2,0,1:T(1,128)} %get-tuple-element.37), channel_id=1, source_target_pairs={{1,0},{2,1},{3,2},{5,4},{6,5},{7,6},{9,8},{10,9},{11,10},{13,12},{... | collective-permute-start | bytes 12296 | tf_op jit(solution)/shard_map/ppermute | solution.py:17
  31.3 3.0 %copy-start.7 = (f32[1,1,6,2048]{3,1,2,0:T(1,128)S(1)}, f32[1,1,6,2048]{3,1,2,0:T(1,128)}, u32[]{:S(2)}) copy-start(f32[1,1,6,2048]{3,1,2,0:T(1,128)} %param.21) | copy-start | bytes 147460
  34.2 20.6 %copy-start.39 = (s32[32]{0:T(128)}, s32[32]{0:T(128)S(1)}, u32[]{:S(2)}) copy-start(s32[32]{0:T(128)S(1)} %eq.543) | copy-start | bytes 388
  34.3 20.3 %collective-permute-start.1 = (bf16[1,2,128,128]{3,2,1,0:T(8,128)(2,1)S(1)}, bf16[1,2,128,128]{3,2,1,0:T(8,128)(2,1)S(1)}, u32[]{:S(2)}, u32[]{:S(2)}) collective-permute-start(bf16[1,2,128,128]{3,2,1,0:T(8,128)(2,1)S(1)} %copy.107), channel_id=1, source_target_pairs={{4,0},{8,4},{12,8},{16,12},{20,16},{24,20},{28,24},{32,28},{36,32}... | collective-permute-start | bytes 196616 | tf_op jit(solution)/shard_map/ppermute | solution.py:17
  36.8 17.8 %collective-permute-start.2 = (bf16[1,2,128,128]{3,2,1,0:T(8,128)(2,1)S(1)}, bf16[1,2,128,128]{3,2,1,0:T(8,128)(2,1)S(1)}, u32[]{:S(2)}, u32[]{:S(2)}) collective-permute-start(bf16[1,2,128,128]{3,2,1,0:T(8,128)(2,1)S(1)} %copy.106), channel_id=1, source_target_pairs={{0,1},{1,2},{2,3},{4,5},{5,6},{6,7},{8,9},{9,10},{10,11},{12,13},{... | collective-permute-start | bytes 196616 | tf_op jit(solution)/shard_map/ppermute | solution.py:14
  40.2 14.4 %collective-permute-start.3 = (bf16[1,2,128,128]{3,2,1,0:T(8,128)(2,1)S(1)}, bf16[1,2,128,128]{3,2,1,0:T(8,128)(2,1)S(1)}, u32[]{:S(2)}, u32[]{:S(2)}) collective-permute-start(bf16[1,2,128,128]{3,2,1,0:T(8,128)(2,1)S(1)} %copy.105), channel_id=1, source_target_pairs={{1,0},{2,1},{3,2},{5,4},{6,5},{7,6},{9,8},{10,9},{11,10},{13,12},{... | collective-permute-start | bytes 196616 | tf_op jit(solution)/shard_map/ppermute | solution.py:17
  43.1 8.8 %copy-start.12 = (f32[1,4,24,128]{3,1,2,0:T(4,128)}, f32[1,4,24,128]{3,1,2,0:T(4,128)S(1)}, u32[]{:S(2)}) copy-start(f32[1,4,24,128]{3,1,2,0:T(4,128)S(1)} %maximum_bitcast_fusion) | copy-start | bytes 147460
  43.1 3.4 %copy-start.4 = (f32[2048,128]{0,1:T(8,128)S(1)}, f32[2048,128]{0,1:T(8,128)}, u32[]{:S(2)}) copy-start(f32[2048,128]{0,1:T(8,128)} %fusion.36) | copy-start | bytes 3145732
  43.1 3.4 %copy-start.33 = (s32[2048]{0:T(1024)S(1)}, s32[2048]{0:T(1024)}, u32[]{:S(2)}) copy-start(s32[2048]{0:T(1024)} %get-tuple-element.42) | copy-start | bytes 24580
  46.5 2.7 %copy-start.5 = (f32[2048,128]{0,1:T(8,128)S(1)}, f32[2048,128]{0,1:T(8,128)}, u32[]{:S(2)}) copy-start(f32[2048,128]{0,1:T(8,128)} %fusion.35) | copy-start | bytes 3145732
  46.5 2.7 %copy-start.34 = (s32[2048]{0:T(1024)S(1)}, s32[2048]{0:T(1024)}, u32[]{:S(2)}) copy-start(s32[2048]{0:T(1024)} %get-tuple-element.44) | copy-start | bytes 24580
  49.2 2.7 %copy-start.6 = (f32[2048,128]{0,1:T(8,128)S(1)}, f32[2048,128]{0,1:T(8,128)}, u32[]{:S(2)}) copy-start(f32[2048,128]{0,1:T(8,128)} %fusion.34) | copy-start | bytes 3145732
  49.2 2.7 %copy-start.35 = (s32[2048]{0:T(1024)S(1)}, s32[2048]{0:T(1024)}, u32[]{:S(2)}) copy-start(s32[2048]{0:T(1024)} %get-tuple-element.46) | copy-start | bytes 24580
  55.3 1.7 %copy-start.2 = (bf16[1,1,16,128,128]{4,3,2,1,0:T(8,128)(2,1)S(1)}, bf16[1,1,16,128,128]{4,3,2,1,0:T(8,128)(2,1)}, u32[]{:S(2)}) copy-start(bf16[1,1,16,128,128]{4,3,2,1,0:T(8,128)(2,1)} %param.16) | copy-start | bytes 1572868
  57.1 2.0 %copy-start.38 = (s32[8]{0:T(128)S(1)}, s32[8]{0:T(128)}, u32[]{:S(2)}) copy-start(s32[8]{0:T(128)} %copy-done.37) | copy-start | bytes 100
  59.1 15.2 %copy-start.3 = (f32[2048,128]{0,1:T(8,128)S(1)}, f32[2048,128]{0,1:T(8,128)}, u32[]{:S(2)}) copy-start(f32[2048,128]{0,1:T(8,128)} %fusion.33) | copy-start | bytes 3145732
  59.1 15.2 %copy-start.13 = (f32[1,4,24,128]{3,1,2,0:T(4,128)S(1)}, f32[1,4,24,128]{3,1,2,0:T(4,128)}, u32[]{:S(2)}) copy-start(f32[1,4,24,128]{3,1,2,0:T(4,128)} %copy-done.12) | copy-start | bytes 147460
  59.1 15.2 %copy-start.32 = (s32[2048]{0:T(1024)S(1)}, s32[2048]{0:T(1024)}, u32[]{:S(2)}) copy-start(s32[2048]{0:T(1024)} %get-tuple-element.48) | copy-start | bytes 24580
  59.7 17.0 %collective-permute-start.4 = (bf16[1,2,128,128]{3,2,1,0:T(8,128)(2,1)S(1)}, bf16[1,2,128,128]{3,2,1,0:T(8,128)(2,1)S(1)}, u32[]{:S(2)}, u32[]{:S(2)}) collective-permute-start(bf16[1,2,128,128]{3,2,1,0:T(8,128)(2,1)S(1)} %copy.104), channel_id=1, source_target_pairs={{0,4},{4,8},{8,12},{12,16},{16,20},{20,24},{24,28},{28,32},{32,36}... | collective-permute-start | bytes 196616 | tf_op jit(solution)/shard_map/ppermute | solution.py:14
  66.8 10.0 %collective-permute-start.5 = (bf16[1,2,128,128]{3,2,1,0:T(8,128)(2,1)S(1)}, bf16[1,2,128,128]{3,2,1,0:T(8,128)(2,1)S(1)}, u32[]{:S(2)}, u32[]{:S(2)}) collective-permute-start(bf16[1,2,128,128]{3,2,1,0:T(8,128)(2,1)S(1)} %copy.103), channel_id=1, source_target_pairs={{4,0},{8,4},{12,8},{16,12},{20,16},{24,20},{28,24},{32,28},{36,32}... | collective-permute-start | bytes 196616 | tf_op jit(solution)/shard_map/ppermute | solution.py:17
  68.7 8.1 %collective-permute-start.6 = (bf16[1,2,128,128]{3,2,1,0:T(8,128)(2,1)S(1)}, bf16[1,2,128,128]{3,2,1,0:T(8,128)(2,1)S(1)}, u32[]{:S(2)}, u32[]{:S(2)}) collective-permute-start(bf16[1,2,128,128]{3,2,1,0:T(8,128)(2,1)S(1)} %copy.102), channel_id=1, source_target_pairs={{0,1},{1,2},{2,3},{4,5},{5,6},{6,7},{8,9},{9,10},{10,11},{12,13},{... | collective-permute-start | bytes 196616 | tf_op jit(solution)/shard_map/ppermute | solution.py:14
  72.1 5.0 %collective-permute-start.7 = (bf16[1,2,128,128]{3,2,1,0:T(8,128)(2,1)S(1)}, bf16[1,2,128,128]{3,2,1,0:T(8,128)(2,1)S(1)}, u32[]{:S(2)}, u32[]{:S(2)}) collective-permute-start(bf16[1,2,128,128]{3,2,1,0:T(8,128)(2,1)S(1)} %copy.101), channel_id=1, source_target_pairs={{1,0},{2,1},{3,2},{5,4},{6,5},{7,6},{9,8},{10,9},{11,10},{13,12},{... | collective-permute-start | bytes 196616 | tf_op jit(solution)/shard_map/ppermute | solution.py:17
  78.1 20.6 %copy-start.31 = (s32[2048]{0:T(1024)S(1)}, s32[2048]{0:T(1024)}, u32[]{:S(2)}) copy-start(s32[2048]{0:T(1024)} %get-tuple-element.62) | copy-start | bytes 24580
  82.5 22.5 %copy-start.19 = (s32[2048]{0:T(1024)S(1)}, s32[2048]{0:T(1024)}, u32[]{:S(2)}) copy-start(s32[2048]{0:T(1024)} %get-tuple-element.50) | copy-start | bytes 24580
  82.5 22.5 %copy-start.20 = (s32[2048]{0:T(1024)S(1)}, s32[2048]{0:T(1024)}, u32[]{:S(2)}) copy-start(s32[2048]{0:T(1024)} %get-tuple-element.51) | copy-start | bytes 24580
  82.5 20.2 %collective-permute-start.10 = (bf16[1,2,1,128]{3,1,2,0:T(2,128)(2,1)S(1)}, bf16[1,2,1,128]{3,1,2,0:T(2,128)(2,1)S(1)}, u32[]{:S(2)}, u32[]{:S(2)}) collective-permute-start(bf16[1,2,1,128]{3,1,2,0:T(2,128)(2,1)S(1)} %get-tuple-element.11), channel_id=1, source_target_pairs={{0,1},{1,2},{2,3},{4,5},{5,6},{6,7},{8,9},{9,10},{10,11},{12,13},{... | collective-permute-start | bytes 1544 | tf_op jit(solution)/shard_map/ppermute | solution.py:14
  85.6 17.2 %collective-permute-start.11 = (bf16[1,2,1,128]{3,1,2,0:T(2,128)(2,1)S(1)}, bf16[1,2,1,128]{3,1,2,0:T(2,128)(2,1)S(1)}, u32[]{:S(2)}, u32[]{:S(2)}) collective-permute-start(bf16[1,2,1,128]{3,1,2,0:T(2,128)(2,1)S(1)} %get-tuple-element.10), channel_id=1, source_target_pairs={{1,0},{2,1},{3,2},{5,4},{6,5},{7,6},{9,8},{10,9},{11,10},{13,12},{... | collective-permute-start | bytes 1544 | tf_op jit(solution)/shard_map/ppermute | solution.py:17
  87.8 15.0 %collective-permute-start.8 = (bf16[1,2,1,128]{3,1,2,0:T(2,128)(2,1)S(1)}, bf16[1,2,1,128]{3,1,2,0:T(2,128)(2,1)S(1)}, u32[]{:S(2)}, u32[]{:S(2)}) collective-permute-start(bf16[1,2,1,128]{3,1,2,0:T(2,128)(2,1)S(1)} %get-tuple-element.9), channel_id=1, source_target_pairs={{0,4},{4,8},{8,12},{12,16},{16,20},{20,24},{24,28},{28,32},{32,36}... | collective-permute-start | bytes 1544 | tf_op jit(solution)/shard_map/ppermute | solution.py:14
  96.8 8.2 %collective-permute-start.9 = (bf16[1,2,1,128]{3,1,2,0:T(2,128)(2,1)S(1)}, bf16[1,2,1,128]{3,1,2,0:T(2,128)(2,1)S(1)}, u32[]{:S(2)}, u32[]{:S(2)}) collective-permute-start(bf16[1,2,1,128]{3,1,2,0:T(2,128)(2,1)S(1)} %get-tuple-element.12), channel_id=1, source_target_pairs={{4,0},{8,4},{12,8},{16,12},{20,16},{24,20},{28,24},{32,28},{36,32}... | collective-permute-start | bytes 1544 | tf_op jit(solution)/shard_map/ppermute | solution.py:17
  102.0 3.7 %copy-start.21 = (s32[2048]{0:T(1024)S(1)}, s32[2048]{0:T(1024)}, u32[]{:S(2)}) copy-start(s32[2048]{0:T(1024)} %get-tuple-element.52) | copy-start | bytes 24580
  102.0 3.7 %copy-start.22 = (s32[2048]{0:T(1024)S(1)}, s32[2048]{0:T(1024)}, u32[]{:S(2)}) copy-start(s32[2048]{0:T(1024)} %get-tuple-element.53) | copy-start | bytes 24580
  105.0 1.3 %copy-start.23 = (s32[2048]{0:T(1024)S(1)}, s32[2048]{0:T(1024)}, u32[]{:S(2)}) copy-start(s32[2048]{0:T(1024)} %get-tuple-element.54) | copy-start | bytes 24580
  105.0 1.3 %copy-start.24 = (s32[2048]{0:T(1024)S(1)}, s32[2048]{0:T(1024)}, u32[]{:S(2)}) copy-start(s32[2048]{0:T(1024)} %get-tuple-element.55) | copy-start | bytes 24580
  105.7 1.3 %copy-start.25 = (s32[2048]{0:T(1024)S(1)}, s32[2048]{0:T(1024)}, u32[]{:S(2)}) copy-start(s32[2048]{0:T(1024)} %get-tuple-element.56) | copy-start | bytes 24580
  105.7 1.3 %copy-start.26 = (s32[2048]{0:T(1024)S(1)}, s32[2048]{0:T(1024)}, u32[]{:S(2)}) copy-start(s32[2048]{0:T(1024)} %get-tuple-element.57) | copy-start | bytes 24580
  106.4 1.3 %copy-start.27 = (s32[2048]{0:T(1024)S(1)}, s32[2048]{0:T(1024)}, u32[]{:S(2)}) copy-start(s32[2048]{0:T(1024)} %get-tuple-element.58) | copy-start | bytes 24580
  107.0 1.4 %copy-start.29 = (s32[2048]{0:T(1024)S(1)}, s32[2048]{0:T(1024)}, u32[]{:S(2)}) copy-start(s32[2048]{0:T(1024)} %get-tuple-element.60) | copy-start | bytes 24580
  107.0 1.4 %copy-start.30 = (s32[2048]{0:T(1024)S(1)}, s32[2048]{0:T(1024)}, u32[]{:S(2)}) copy-start(s32[2048]{0:T(1024)} %get-tuple-element.61) | copy-start | bytes 24580
  (10 other events, 9.9 us)
where the time goes:
time: 111 us; the launch traced here: 110 us
  starting transfers between devices  53.2 us (48%)
  matrix products  29.6 us (27%)
  other arithmetic  16.1 us (15%)
  local copies, waits for them, and re-layouts  6.97 us (6%)
  waiting for transfers between devices  2.6 us (2%)
  between operations  1.74 us (2%)
    ppermute x8, starting transfers between devices, with_halo(): lax.ppermute(lax.slice_in_dim(block, block.shape[dim] - width, None, axis...  35.5 us
    dot_general x13, matrix products, lookup(): jnp.einsum('nh,mhl->mnl', high_hot, table, precision=lax.Precision.HIGHES...  21.5 us
    ppermute x8, starting transfers between devices, with_halo(): lax.ppermute(lax.slice_in_dim(block, 0, width, axis=dim), axis, backward)  17.7 us
    convert_element_type x7, other arithmetic, lookup(): (low_part[:, None] == lax.broadcasted_iota(jnp.int32, (1, lane_width), 1)...  5.61 us
    unnamed x105, local copies, waits for them, and re-layouts  5.28 us
    dot_general x2, matrix products, smooth(): jnp.einsum('bij,brj->bri', inverse, resid, preferred_element_type=jnp.flo...  4.94 us
    sub x6, other arithmetic, lookup(): low_part = index - high_part * lane_width  3.71 us
    select_n x7, other arithmetic, lookup(): high_part = index // lane_width  3.64 us
  transfers between devices with their start and end apart: 16, of which 2 were waited for; matrix products, arithmetic and copies ran while one was open for 31% of the time, Pallas kernels for 0%

commit v1 on v0

v1 whole, which is shorter than its diff:
```python
import functools

import jax
import jax.numpy as jnp
from jax import lax
from jax.experimental import pallas as pl
from jax.experimental.pallas import tpu as pltpu
from jax.sharding import PartitionSpec as P

MESH = pl.DeviceIdType.MESH
LANES = 128
CHUNKS = ((0, 64), (64, 64))

OPPOSITE = (1, 0, 3, 2)


def nt_dot(a, b):
    return lax.dot_general(a, b, (((1,), (1,)), ((), ())), preferred_element_type=jnp.float32)


def pick_lanes(index, rows):
    low = index % LANES
    group = index // LANES
    result = jnp.zeros(index.shape, jnp.float32)
    for at, row in enumerate(rows):
        spread = jnp.broadcast_to(row, index.shape)
        taken = jnp.take_along_axis(spread, low, axis=1, mode="promise_in_bounds")
        result = jnp.where(group == at, taken, result)
    return result


def kernel(
    n_wide,
    n_narrow,
    links,
    sends,
    guess_hbm,
    rhs_hbm,
    inverse_hbm,
    couple_hbm,
    faces_hbm,
    coeff_hbm,
    source_hbm,
    near_hbm,
    flags_hbm,
    outbound_hbm,
    modes_hbm,
    ratio_hbm,
    traces_out,
    modes_out,
    guess,
    rhs,
    inverse,
    couple,
    faces,
    coeff,
    source,
    near,
    flags,
    outbound,
    modes,
    ratio,
    traces,
    modes_next,
    tables,
    cell_table,
    cell_out,
    cell_in,
    face_own,
    face_out,
    face_in,
    upwind,
    *rest,
):
    count = len(CHUNKS)
    first_ext, rest = rest[:count], rest[count:]
    second_ext, rest = rest[:count], rest[count:]
    second_own, rest = rest[:count], rest[count:]
    first_out, rest = rest[:count], rest[count:]
    second_out, rest = rest[:count], rest[count:]
    load_sem, store_sem, send_sem, recv_sem = rest
    blocks = guess.shape[0]
    halo = sends.shape[0]

    i = lax.axis_index("wide")
    j = lax.axis_index("narrow")
    there = (i > 0, i < n_wide - 1, j > 0, j < n_narrow - 1)
    device = ((i - 1, j), (i + 1, j), (i, j - 1), (i, j + 1))

    loads = []
    for at, (src, dst) in enumerate(
        (
            (guess_hbm, guess),
            (modes_hbm, modes),
            (outbound_hbm, outbound),
            (couple_hbm, couple),
            (rhs_hbm, rhs),
            (inverse_hbm, inverse),
            (near_hbm, near),
            (flags_hbm, flags),
            (faces_hbm, faces),
            (coeff_hbm, coeff),
            (source_hbm, source),
            (ratio_hbm, ratio),
        )
    ):
        copy = pltpu.make_async_copy(src, dst, load_sem.at[at])
        copy.start()
        loads.append(copy)

    barrier = pltpu.get_barrier_semaphore()
    for side in range(4):

        @pl.when(there[side])
        def _():
            pl.semaphore_signal(barrier, inc=1, device_id=device[side], device_id_type=MESH)

    def remote(src, dst, slot, side):
        return pltpu.make_async_remote_copy(
            src_ref=src,
            dst_ref=dst,
            send_sem=send_sem.at[slot, side],
            recv_sem=recv_sem.at[slot, side],
            device_id=device[side],
            device_id_type=MESH,
        )

    def start(slot, source_of, target_of):
        for side in range(4):

            @pl.when(there[side])
            def _():
                remote(source_of(side), target_of(OPPOSITE[side]), slot, side).start()

    def wait_sent(slot, source_of, target_of):
        for side in range(4):

            @pl.when(there[side])
            def _():
                remote(source_of(side), target_of(OPPOSITE[side]), slot, side).wait_send()

    def wait_arrived(slot, source_of, target_of):
        for side in range(4):

            @pl.when(there[side])
            def _():
                remote(source_of(side), target_of(side), slot, OPPOSITE[side]).wait_recv()

    def block_refs(outgoing, extended):
        return (
            lambda side: outgoing.at[pl.ds(side * halo, halo)],
            lambda side: extended.at[pl.ds(blocks + side * halo, halo)],
        )

    for part in range(count):
        for side in range(4):

            @pl.when(jnp.logical_not(there[side]))
            def _():
                at = pl.ds(blocks + side * halo, halo)
                empty = jnp.zeros((halo,) + first_ext[part].shape[1:], jnp.bfloat16)
                first_ext[part][at] = empty
                second_ext[part][at] = empty

    for side in range(4):

        @pl.when(jnp.logical_not(there[side]))
        def _():
            cell_in[side] = jnp.zeros(cell_in.shape[1:], jnp.float32)
            face_in[side] = jnp.zeros(face_in.shape[1:], jnp.float32)

    loads[0].wait()
    for part, (low, size) in enumerate(CHUNKS):
        for side in range(4):
            for h in range(halo):
                picked = guess[sends[h, side], low : low + size, :]
                first_out[part][side * halo + h] = picked.astype(jnp.bfloat16)
    neighbours = sum(x.astype(jnp.int32) for x in there)
    pl.semaphore_wait(barrier, neighbours)
    for part in range(count):
        start(part, *block_refs(first_out[part], first_ext[part]))

    cell_slot, face_slot = 2 * count, 2 * count + 1
    loads[1].wait()
    loads[2].wait()
    groups = modes.shape[0] // 4
    mode = [modes[pl.ds(m, groups, stride=4), :] for m in range(4)]
    for face in range(6):
        slope = mode[face // 2 + 1]
        table = mode[0] + slope if face % 2 == 0 else mode[0] - slope
        tables[face] = table
        if face < 4:
            cell_table[pl.ds(OPPOSITE[face], groups, stride=8), :] = table
            cell_table[pl.ds(OPPOSITE[face] + 4, groups, stride=8), :] = table
    index = outbound[...]
    low_part, high_part = index % LANES, index // LANES
    sent = jnp.zeros(index.shape, jnp.float32)
    for at in range(groups):
        taken = jnp.take_along_axis(
            cell_table[8 * at : 8 * at + 8, :], low_part, axis=1, mode="promise_in_bounds"
        )
        sent = jnp.where(high_part == at, taken, sent)
    for side in range(4):
        for h in range(2):
            cell_out[side, h : h + 1, :] = sent[4 * h + side : 4 * h + side + 1, :]
    cell_refs = (lambda side: cell_out.at[side], lambda side: cell_in.at[side])
    start(cell_slot, *cell_refs)

    for part, (low, size) in enumerate(CHUNKS):
        for b in range(blocks):
            first_ext[part][b] = guess[b, low : low + size, :].astype(jnp.bfloat16)

    loads[6].wait()
    loads[7].wait()
    wait_arrived(cell_slot, *cell_refs)
    for face in range(6):
        at = slice(face * groups, (face + 1) * groups)
        index = near[at, :]
        own = mode[0] - mode[face // 2 + 1] if face % 2 == 0 else mode[0] + mode[face // 2 + 1]
        rows = [tables[face, g : g + 1, :] for g in range(groups)]
        if face < 4:
            rows = rows + [cell_in[face, h : h + 1, :] for h in range(2)]
            index = jnp.where(index < groups * LANES, index, index - face * 2 * LANES)
        across = pick_lanes(index, rows)
        upwind[at, :] = jnp.where(flags[at, :] == 1, own, across)

    def smooth(extended, low, size, b):
        pair = jnp.concatenate([extended[links[0, b]], extended[links[1, b]]], axis=1)
        weight = jnp.concatenate([couple[b, 0], couple[b, 1]], axis=1)
        coupled = nt_dot(pair, weight)
        resid = (rhs[b, low : low + size, :] - coupled).astype(jnp.bfloat16)
        return nt_dot(resid, inverse[b])

    loads[3].wait()
    loads[4].wait()
    loads[5].wait()
    for part, (low, size) in enumerate(CHUNKS):
        wait_arrived(part, *block_refs(first_out[part], first_ext[part]))
        for b in range(blocks):
            new = smooth(first_ext[part], low, size, b).astype(jnp.bfloat16)
            second_own[part][b] = new
            second_ext[part][b] = new
        for side in range(4):
            for h in range(halo):
                second_out[part][side * halo + h] = second_own[part][sends[h, side]]
        start(count + part, *block_refs(second_out[part], second_ext[part]))

    face_refs = (lambda side: face_out.at[side], lambda side: face_in.at[side])
    stores = []
    for part, (low, size) in enumerate(CHUNKS):
        wait_arrived(count + part, *block_refs(second_out[part], second_ext[part]))
        for b in range(blocks):
            new = smooth(second_ext[part], low, size, b)
            traces[b, low : low + size, :] = new
            if part == 0:
                face_own[b] = new[0:1, :].astype(jnp.bfloat16).astype(jnp.float32)
        if part == 0:
            for side in range(4):
                for h in range(halo):
                    face_out[side, h : h + 1, :] = face_own[sends[h, side]]
            start(face_slot, *face_refs)
        copy = pltpu.make_async_copy(
            traces.at[:, pl.ds(low, size), :], traces_out.at[:, pl.ds(low, size), :], store_sem.at[part]
        )
        copy.start()
        stores.append(copy)

    for at in range(8, 12):
        loads[at].wait()
    wait_arrived(face_slot, *face_refs)
    rows = [face_own[b] for b in range(blocks)]
    rows = rows + [face_in[side, h : h + 1, :] for side in range(4) for h in range(halo)]
    face_trace = pick_lanes(faces[...], rows)
    weights = [coeff[f * groups : (f + 1) * groups, :] for f in range(6)]
    values = [face_trace[f * groups : (f + 1) * groups, :] for f in range(6)]
    total = sum(weights[1:], weights[0])
    weighted = [w * v for w, v in zip(weights, values)]
    pressure = (source[...] + sum(weighted[1:], weighted[0])) / total
    flux = [w * (pressure - v) for w, v in zip(weights, values)]
    flow = [flux[f] * upwind[f * groups : (f + 1) * groups, :] for f in range(6)]
    step = ratio[...]
    modes_next[pl.ds(0, groups, stride=4), :] = mode[0] - step * sum(flow[1:], flow[0])
    for m in range(1, 4):
        lo, hi = 2 * m - 2, 2 * m - 1
        volume = 0.5 * (flux[hi] - flux[lo]) * mode[0]
        modes_next[pl.ds(m, groups, stride=4), :] = mode[m] + 3.0 * step * (
            volume - (flow[hi] - flow[lo])
        )
    copy = pltpu.make_async_copy(modes_next, modes_out, store_sem.at[count])
    copy.start()
    stores.append(copy)

    for part in range(count):
        wait_sent(part, *block_refs(first_out[part], first_ext[part]))
        wait_sent(count + part, *block_refs(second_out[part], second_ext[part]))
    wait_sent(cell_slot, *cell_refs)
    wait_sent(face_slot, *face_refs)
    for copy in stores:
        copy.wait()


def per_device(
    n_wide,
    n_narrow,
    trace_guess,
    trace_rhs,
    block_inverse,
    coupling,
    block_neighbours,
    block_send,
    cell_faces,
    face_coeff,
    cell_source,
    cell_neighbours,
    upwind_flags,
    cell_send,
    saturation,
    step_ratio,
):
    blocks, rows, width = trace_guess.shape[2:]
    halo = block_send.shape[3]
    cells = saturation.shape[3]
    groups = cells // LANES
    side_groups = cell_send.shape[3] // LANES

    def by_tile(x):
        modes, length = x.shape[2:]
        return x.reshape(modes, length // LANES, LANES).transpose(1, 0, 2).reshape(-1, LANES)

    operands = (
        block_neighbours[0, 0].T,
        block_send[0, 0].T,
        trace_guess[0, 0],
        trace_rhs[0, 0],
        block_inverse[0, 0],
        coupling[0, 0],
        cell_faces.reshape(-1, LANES),
        face_coeff.reshape(-1, LANES),
        cell_source.reshape(-1, LANES),
        cell_neighbours.reshape(-1, LANES),
        upwind_flags.reshape(-1, LANES),
        by_tile(cell_send),
        by_tile(saturation),
        step_ratio.reshape(-1, LANES),
    )
    f32, bf16 = jnp.float32, jnp.bfloat16
    extended = blocks + 4 * halo
    slots = 2 * len(CHUNKS) + 2
    scratch = [pltpu.VMEM(x.shape, x.dtype) for x in operands[2:]]
    scratch += [
        pltpu.VMEM((blocks, rows, width), f32),
        pltpu.VMEM((4 * groups, LANES), f32),
        pltpu.VMEM((6, groups, LANES), f32),
        pltpu.VMEM((8 * groups, LANES), f32),
        pltpu.VMEM((4, side_groups, LANES), f32),
        pltpu.VMEM((4, side_groups, LANES), f32),
        pltpu.VMEM((blocks, 1, width), f32),
        pltpu.VMEM((4, halo, width), f32),
        pltpu.VMEM((4, halo, width), f32),
        pltpu.VMEM((6 * groups, LANES), f32),
    ]
    for leading in (extended, extended, blocks, 4 * halo, 4 * halo):
        scratch += [pltpu.VMEM((leading, size, width), bf16) for _, size in CHUNKS]
    scratch += [
        pltpu.SemaphoreType.DMA((12,)),
        pltpu.SemaphoreType.DMA((len(CHUNKS) + 1,)),
        pltpu.SemaphoreType.DMA((slots, 4)),
        pltpu.SemaphoreType.DMA((slots, 4)),
    ]
    traces, modes = pl.pallas_call(
        functools.partial(kernel, n_wide, n_narrow),
        out_shape=(
            jax.ShapeDtypeStruct((blocks, rows, width), f32),
            jax.ShapeDtypeStruct((4 * groups, LANES), f32),
        ),
        in_specs=[pl.BlockSpec(memory_space=pltpu.SMEM)] * 2
        + [pl.BlockSpec(memory_space=pltpu.HBM)] * 12,
        out_specs=(pl.BlockSpec(memory_space=pl.ANY),) * 2,
        scratch_shapes=scratch,
        compiler_params=pltpu.CompilerParams(
            collective_id=0, has_side_effects=True, vmem_limit_bytes=32 * 1024 * 1024
        ),
        name="smooth_and_section",
    )(*operands)
    modes = modes.reshape(groups, 4, LANES).transpose(1, 0, 2).reshape(1, 1, 4, cells)
    return traces[None, None], modes


def solution(mesh):
    def placed(rank):
        return P("wide", "narrow", *([None] * (rank - 2)))

    ranks = (5, 5, 5, 6, 4, 4, 4, 4, 3, 4, 4, 4, 4, 3)
    return jax.shard_map(
        functools.partial(per_device, mesh.shape["wide"], mesh.shape["narrow"]),
        mesh=mesh,
        in_specs=tuple(placed(rank) for rank in ranks),
        out_specs=(placed(5), placed(4)),
        check_vma=False,
    )
```

time: 111 us -> 33.6 us (0.30)
  the two profiles are of different devices: /device:TPU:253 before, /device:TPU:386 now
where the time goes in v1:
time: 33.6 us; the launch traced here: 33 us
  Pallas kernels  21.3 us (63%)
  local copies, waits for them, and re-layouts  11 us (33%)
  between operations  0.7 us (2%)
    pallas_call x1, Pallas kernels, per_device(): pl.pallas_call(functools.partial(kernel, n_wide, n_narrow), out_shape=(ja...  21.3 us
    unnamed x30, local copies, waits for them, and re-layouts  11 us

profile of v1, /device:TPU:386, one launch (start us, length us, event | category | flops | bytes accessed | tf_op | source)
XLA Modules:
  0.0 33.0 jit_solution(9447914323836718937)
XLA Ops:
  0.6 0.0 copy-start.12
  0.6 0.0 copy-start.13
  0.7 0.0 copy-start.11
  0.7 0.0 copy-start.10
  0.7 0.0 copy-start.9
  0.7 0.6 %copy-done.12 = s32[1,1,16,2]{2,3,1,0:T(2,128)S(1)} copy-done((s32[1,1,16,2]{2,3,1,0:T(2,128)S(1)}, s32[1,1,16,2]{2,3,1,0:T(2,128)}, u32[]{:S(2)}) %copy-start.12) | copy-done | bytes 152
  1.3 0.0 copy-done.13
  1.3 0.0 copy-done.11
  1.4 0.0 copy-done.10
  1.4 0.0 copy-done.9
  1.4 0.0 copy-start
  1.4 1.2 %copy-done = f32[1,1,16,128,128]{4,3,2,1,0:T(8,128)S(1)} copy-done((f32[1,1,16,128,128]{4,3,2,1,0:T(8,128)S(1)}, f32[1,1,16,128,128]{4,3,2,1,0:T(8,128)}, u32[]{:S(2)}) %copy-start) | copy-done | bytes 1048600
  2.6 0.0 copy-start.1
  2.6 1.2 %copy-done.1 = f32[1,1,16,128,128]{4,3,2,1,0:T(8,128)S(1)} copy-done((f32[1,1,16,128,128]{4,3,2,1,0:T(8,128)S(1)}, f32[1,1,16,128,128]{4,3,2,1,0:T(8,128)}, u32[]{:S(2)}) %copy-start.1) | copy-done | bytes 1048600
  3.8 0.0 copy-start.2
  3.9 1.2 %copy-done.2 = bf16[1,1,16,2,128,128]{5,4,3,2,1,0:T(8,128)(2,1)S(1)} copy-done((bf16[1,1,16,2,128,128]{5,4,3,2,1,0:T(8,128)(2,1)S(1)}, bf16[1,1,16,2,128,128]{5,4,3,2,1,0:T(8,128)(2,1)}, u32[]{:S(2)}) %copy-start.2) | copy-done | bytes 1048600
  5.1 0.0 copy-start.3
  5.1 1.0 %copy-done.3 = bf16[1,1,16,128,128]{4,3,2,1,0:T(8,128)(2,1)S(1)} copy-done((bf16[1,1,16,128,128]{4,3,2,1,0:T(8,128)(2,1)S(1)}, bf16[1,1,16,128,128]{4,3,2,1,0:T(8,128)(2,1)}, u32[]{:S(2)}) %copy-start.3) | copy-done | bytes 524312
  6.1 0.0 copy-start.4
  6.1 0.8 %copy-done.4 = s32[1,1,6,2048]{3,1,2,0:T(1,128)S(1)} copy-done((s32[1,1,6,2048]{3,1,2,0:T(1,128)S(1)}, s32[1,1,6,2048]{3,1,2,0:T(1,128)}, u32[]{:S(2)}) %copy-start.4) | copy-done | bytes 49176
  6.9 0.0 copy-start.5
  6.9 0.8 %copy-done.5 = f32[1,1,6,2048]{3,1,2,0:T(1,128)S(1)} copy-done((f32[1,1,6,2048]{3,1,2,0:T(1,128)S(1)}, f32[1,1,6,2048]{3,1,2,0:T(1,128)}, u32[]{:S(2)}) %copy-start.5) | copy-done | bytes 49176
  7.7 0.0 copy-start.6
  7.7 0.8 %copy-done.6 = s32[1,1,6,2048]{3,1,2,0:T(1,128)S(1)} copy-done((s32[1,1,6,2048]{3,1,2,0:T(1,128)S(1)}, s32[1,1,6,2048]{3,1,2,0:T(1,128)}, u32[]{:S(2)}) %copy-start.6) | copy-done | bytes 49176
  8.5 0.0 copy-start.7
  8.5 0.8 %copy-done.7 = s32[1,1,6,2048]{3,1,2,0:T(1,128)S(1)} copy-done((s32[1,1,6,2048]{3,1,2,0:T(1,128)S(1)}, s32[1,1,6,2048]{3,1,2,0:T(1,128)}, u32[]{:S(2)}) %copy-start.7) | copy-done | bytes 49176
  9.3 0.0 copy-start.8
  9.3 0.8 %copy-done.8 = f32[1,1,4,2048]{3,2,1,0:T(4,128)S(1)} copy-done((f32[1,1,4,2048]{3,2,1,0:T(4,128)S(1)}, f32[1,1,4,2048]{3,2,1,0:T(4,128)}, u32[]{:S(2)}) %copy-start.8) | copy-done | bytes 32792
  10.1 21.3 %smooth_and_section.1 = (f32[16,128,128]{2,1,0:T(8,128)S(1)}, f32[64,128]{1,0:T(8,128)S(1)}) custom-call(s32[2,16]{1,0:T(2,128)S(1)} %bitcast.46, s32[2,4]{1,0:T(2,128)S(1)} %bitcast.47, f32[16,128,128]{2,1,0:T(8,128)S(1)} %bitcast.33, f32[16,128,128]{2,1,0:T(8,128)S(1)} %bitcast.34, bf16[16,128,128]{2,1,0:T(8,128)(2,1)S(1)} %bitcast.36, ...), custom_call_target="tpu_custom_call" | custom-call | tf_op jit(solution)/shard_map/smooth_and_section/pallas_call | solution.py:370
  31.4 1.0 %copy.21 = f32[1,1,16,128,128]{4,3,2,1,0:T(8,128)} copy(f32[1,1,16,128,128]{4,3,2,1,0:T(8,128)S(1)} %bitcast.32) | data formatting | bytes 2097152
  32.4 0.6 %copy.22 = f32[1,1,4,2048]{3,2,1,0:T(4,128)} copy(f32[1,1,4,2048]{3,2,1,0:T(4,128)S(1)} %bitcast.42) | data formatting | bytes 65536
Async XLA Ops:
  0.6 0.7 %copy-start.12 = (s32[1,1,16,2]{2,3,1,0:T(2,128)S(1)}, s32[1,1,16,2]{2,3,1,0:T(2,128)}, u32[]{:S(2)}) copy-start(s32[1,1,16,2]{2,3,1,0:T(2,128)} %param.18) | copy-start | bytes 388
  0.6 0.7 %copy-start.13 = (s32[1,1,4,2]{2,3,1,0:T(2,128)S(1)}, s32[1,1,4,2]{2,3,1,0:T(2,128)}, u32[]{:S(2)}) copy-start(s32[1,1,4,2]{2,3,1,0:T(2,128)} %param.19) | copy-start | bytes 100
  0.7 0.7 %copy-start.11 = (s32[1,1,4,256]{3,2,1,0:T(4,128)S(1)}, s32[1,1,4,256]{3,2,1,0:T(4,128)}, u32[]{:S(2)}) copy-start(s32[1,1,4,256]{3,2,1,0:T(4,128)} %param.25) | copy-start | bytes 12292
  0.7 0.7 %copy-start.10 = (f32[1,1,2048]{2,1,0:T(1,128)S(1)}, f32[1,1,2048]{2,1,0:T(1,128)}, u32[]{:S(2)}) copy-start(f32[1,1,2048]{2,1,0:T(1,128)} %param.27) | copy-start | bytes 24580
  0.7 0.7 %copy-start.9 = (f32[1,1,2048]{2,1,0:T(1,128)S(1)}, f32[1,1,2048]{2,1,0:T(1,128)}, u32[]{:S(2)}) copy-start(f32[1,1,2048]{2,1,0:T(1,128)} %param.22) | copy-start | bytes 24580
  1.4 1.2 %copy-start = (f32[1,1,16,128,128]{4,3,2,1,0:T(8,128)S(1)}, f32[1,1,16,128,128]{4,3,2,1,0:T(8,128)}, u32[]{:S(2)}) copy-start(f32[1,1,16,128,128]{4,3,2,1,0:T(8,128)} %param.14) | copy-start | bytes 3145732
  2.6 1.2 %copy-start.1 = (f32[1,1,16,128,128]{4,3,2,1,0:T(8,128)S(1)}, f32[1,1,16,128,128]{4,3,2,1,0:T(8,128)}, u32[]{:S(2)}) copy-start(f32[1,1,16,128,128]{4,3,2,1,0:T(8,128)} %param.15) | copy-start | bytes 3145732
  3.8 1.2 %copy-start.2 = (bf16[1,1,16,2,128,128]{5,4,3,2,1,0:T(8,128)(2,1)S(1)}, bf16[1,1,16,2,128,128]{5,4,3,2,1,0:T(8,128)(2,1)}, u32[]{:S(2)}) copy-start(bf16[1,1,16,2,128,128]{5,4,3,2,1,0:T(8,128)(2,1)} %param.17) | copy-start | bytes 3145732
  5.1 1.0 %copy-start.3 = (bf16[1,1,16,128,128]{4,3,2,1,0:T(8,128)(2,1)S(1)}, bf16[1,1,16,128,128]{4,3,2,1,0:T(8,128)(2,1)}, u32[]{:S(2)}) copy-start(bf16[1,1,16,128,128]{4,3,2,1,0:T(8,128)(2,1)} %param.16) | copy-start | bytes 1572868
  6.1 0.8 %copy-start.4 = (s32[1,1,6,2048]{3,1,2,0:T(1,128)S(1)}, s32[1,1,6,2048]{3,1,2,0:T(1,128)}, u32[]{:S(2)}) copy-start(s32[1,1,6,2048]{3,1,2,0:T(1,128)} %param.20) | copy-start | bytes 147460
  6.9 0.8 %copy-start.5 = (f32[1,1,6,2048]{3,1,2,0:T(1,128)S(1)}, f32[1,1,6,2048]{3,1,2,0:T(1,128)}, u32[]{:S(2)}) copy-start(f32[1,1,6,2048]{3,1,2,0:T(1,128)} %param.21) | copy-start | bytes 147460
  7.7 0.8 %copy-start.6 = (s32[1,1,6,2048]{3,1,2,0:T(1,128)S(1)}, s32[1,1,6,2048]{3,1,2,0:T(1,128)}, u32[]{:S(2)}) copy-start(s32[1,1,6,2048]{3,1,2,0:T(1,128)} %param.23) | copy-start | bytes 147460
  8.5 0.8 %copy-start.7 = (s32[1,1,6,2048]{3,1,2,0:T(1,128)S(1)}, s32[1,1,6,2048]{3,1,2,0:T(1,128)}, u32[]{:S(2)}) copy-start(s32[1,1,6,2048]{3,1,2,0:T(1,128)} %param.24) | copy-start | bytes 147460
  9.3 0.8 %copy-start.8 = (f32[1,1,4,2048]{3,2,1,0:T(4,128)S(1)}, f32[1,1,4,2048]{3,2,1,0:T(4,128)}, u32[]{:S(2)}) copy-start(f32[1,1,4,2048]{3,2,1,0:T(4,128)} %param.26) | copy-start | bytes 98308

commit v2 on v1

--- a/solution.py
+++ b/solution.py
@@ -9,7 +9,8 @@
 
 MESH = pl.DeviceIdType.MESH
 LANES = 128
-CHUNKS = ((0, 64), (64, 64))
+VMEM_LIMIT = 48 * 1024 * 1024
+CHUNKS = ((0, 16), (16, 112))
 
 OPPOSITE = (1, 0, 3, 2)
 
@@ -32,8 +33,8 @@
 def kernel(
     n_wide,
     n_narrow,
-    links,
-    sends,
+    links_hbm,
+    sends_hbm,
     guess_hbm,
     rhs_hbm,
     inverse_hbm,
@@ -46,9 +47,10 @@
     outbound_hbm,
     modes_hbm,
     ratio_hbm,
-    traces_out,
-    modes_out,
-    guess,
+    traces,
+    modes_next,
+    links,
+    sends,
     rhs,
     inverse,
     couple,
@@ -60,8 +62,6 @@
     outbound,
     modes,
     ratio,
-    traces,
-    modes_next,
     tables,
     cell_table,
     cell_out,
@@ -73,13 +73,14 @@
     *rest,
 ):
     count = len(CHUNKS)
+    guess, rest = rest[:count], rest[count:]
     first_ext, rest = rest[:count], rest[count:]
     second_ext, rest = rest[:count], rest[count:]
     second_own, rest = rest[:count], rest[count:]
     first_out, rest = rest[:count], rest[count:]
     second_out, rest = rest[:count], rest[count:]
-    load_sem, store_sem, send_sem, recv_sem = rest
-    blocks = guess.shape[0]
+    load_sem, send_sem, recv_sem = rest
+    blocks = rhs.shape[0]
     halo = sends.shape[0]
 
     i = lax.axis_index("wide")
@@ -87,33 +88,43 @@
     there = (i > 0, i < n_wide - 1, j > 0, j < n_narrow - 1)
     device = ((i - 1, j), (i + 1, j), (i, j - 1), (i, j + 1))
 
-    loads = []
-    for at, (src, dst) in enumerate(
-        (
-            (guess_hbm, guess),
-            (modes_hbm, modes),
-            (outbound_hbm, outbound),
-            (couple_hbm, couple),
-            (rhs_hbm, rhs),
-            (inverse_hbm, inverse),
-            (near_hbm, near),
-            (flags_hbm, flags),
-            (faces_hbm, faces),
-            (coeff_hbm, coeff),
-            (source_hbm, source),
-            (ratio_hbm, ratio),
-        )
-    ):
-        copy = pltpu.make_async_copy(src, dst, load_sem.at[at])
-        copy.start()
-        loads.append(copy)
-
     barrier = pltpu.get_barrier_semaphore()
     for side in range(4):
 
         @pl.when(there[side])
         def _():
             pl.semaphore_signal(barrier, inc=1, device_id=device[side], device_id_type=MESH)
+
+    def load(at, src, dst):
+        copy = pltpu.make_async_copy(src, dst, load_sem.at[at])
+        copy.start()
+        return copy
+
+    load_sends = load(0, sends_hbm, sends)
+    load_guess = []
+    for part, (low, size) in enumerate(CHUNKS):
+        load_guess.append(load(1 + part, guess_hbm.at[:, pl.ds(low, size)], guess[part]))
+    load_links = load(1 + count, links_hbm, links)
+    loads = [
+        load(2 + count + at, src, dst)
+        for at, (src, dst) in enumerate(
+            (
+                (modes_hbm, modes),
+                (outbound_hbm, outbound),
+                (couple_hbm, couple),
+                (rhs_hbm, rhs),
+                (inverse_hbm, inverse),
+                (near_hbm, near),
+                (flags_hbm, flags),
+                (faces_hbm, faces),
+                (coeff_hbm, coeff),
+                (source_hbm, source),
+                (ratio_hbm, ratio),
+            )
+        )
+    ]
+    load_modes, load_outbound, load_couple, load_rhs, load_inverse, load_near, load_flags = loads[:7]
+    load_cells = loads[7:]
 
     def remote(src, dst, slot, side):
         return pltpu.make_async_remote_copy(
@@ -169,20 +180,20 @@
             cell_in[side] = jnp.zeros(cell_in.shape[1:], jnp.float32)
             face_in[side] = jnp.zeros(face_in.shape[1:], jnp.float32)
 
-    loads[0].wait()
+    load_sends.wait()
     for part, (low, size) in enumerate(CHUNKS):
+        load_guess[part].wait()
         for side in range(4):
             for h in range(halo):
-                picked = guess[sends[h, side], low : low + size, :]
+                picked = guess[part][sends[h, side]]
                 first_out[part][side * halo + h] = picked.astype(jnp.bfloat16)
-    neighbours = sum(x.astype(jnp.int32) for x in there)
-    pl.semaphore_wait(barrier, neighbours)
-    for part in range(count):
+        if part == 0:
+            pl.semaphore_wait(barrier, sum(x.astype(jnp.int32) for x in there))
         start(part, *block_refs(first_out[part], first_ext[part]))
 
     cell_slot, face_slot = 2 * count, 2 * count + 1
-    loads[1].wait()
-    loads[2].wait()
+    load_modes.wait()
+    load_outbound.wait()
     groups = modes.shape[0] // 4
     mode = [modes[pl.ds(m, groups, stride=4), :] for m in range(4)]
     for face in range(6):
@@ -208,10 +219,10 @@
 
     for part, (low, size) in enumerate(CHUNKS):
         for b in range(blocks):
-            first_ext[part][b] = guess[b, low : low + size, :].astype(jnp.bfloat16)
-
-    loads[6].wait()
-    loads[7].wait()
+            first_ext[part][b] = guess[part][b].astype(jnp.bfloat16)
+
+    load_near.wait()
+    load_flags.wait()
     wait_arrived(cell_slot, *cell_refs)
     for face in range(6):
         at = slice(face * groups, (face + 1) * groups)
@@ -231,9 +242,10 @@
         resid = (rhs[b, low : low + size, :] - coupled).astype(jnp.bfloat16)
         return nt_dot(resid, inverse[b])
 
-    loads[3].wait()
-    loads[4].wait()
-    loads[5].wait()
+    load_links.wait()
+    load_couple.wait()
+    load_rhs.wait()
+    load_inverse.wait()
     for part, (low, size) in enumerate(CHUNKS):
         wait_arrived(part, *block_refs(first_out[part], first_ext[part]))
         for b in range(blocks):
@@ -246,7 +258,6 @@
         start(count + part, *block_refs(second_out[part], second_ext[part]))
 
     face_refs = (lambda side: face_out.at[side], lambda side: face_in.at[side])
-    stores = []
     for part, (low, size) in enumerate(CHUNKS):
         wait_arrived(count + part, *block_refs(second_out[part], second_ext[part]))
         for b in range(blocks):
@@ -259,14 +270,9 @@
                 for h in range(halo):
                     face_out[side, h : h + 1, :] = face_own[sends[h, side]]
             start(face_slot, *face_refs)
-        copy = pltpu.make_async_copy(
-            traces.at[:, pl.ds(low, size), :], traces_out.at[:, pl.ds(low, size), :], store_sem.at[part]
-        )
-        copy.start()
-        stores.append(copy)
-
-    for at in range(8, 12):
-        loads[at].wait()
+
+    for copy in load_cells:
+        copy.wait()
     wait_arrived(face_slot, *face_refs)
     rows = [face_own[b] for b in range(blocks)]
     rows = rows + [face_in[side, h : h + 1, :] for side in range(4) for h in range(halo)]
@@ -286,16 +292,21 @@
         modes_next[pl.ds(m, groups, stride=4), :] = mode[m] + 3.0 * step * (
             volume - (flow[hi] - flow[lo])
         )
-    copy = pltpu.make_async_copy(modes_next, modes_out, store_sem.at[count])
-    copy.start()
-    stores.append(copy)
-
     for part in range(count):
         wait_sent(part, *block_refs(first_out[part], first_ext[part]))
         wait_sent(count + part, *block_refs(second_out[part], second_ext[part]))
     wait_sent(cell_slot, *cell_refs)
     wait_sent(face_slot, *face_refs)
-    for copy in stores:
+
+
+def write_back(traces, modes, traces_out, modes_out, sem):
+    copies = [
+        pltpu.make_async_copy(traces, traces_out, sem.at[0]),
+        pltpu.make_async_copy(modes, modes_out, sem.at[1]),
+    ]
+    for copy in copies:
+        copy.start()
+    for copy in copies:
         copy.wait()
 
 
@@ -346,10 +357,9 @@
     f32, bf16 = jnp.float32, jnp.bfloat16
     extended = blocks + 4 * halo
     slots = 2 * len(CHUNKS) + 2
-    scratch = [pltpu.VMEM(x.shape, x.dtype) for x in operands[2:]]
+    scratch = [pltpu.SMEM(x.shape, x.dtype) for x in operands[:2]]
+    scratch += [pltpu.VMEM(x.shape, x.dtype) for x in operands[3:]]
     scratch += [
-        pltpu.VMEM((blocks, rows, width), f32),
-        pltpu.VMEM((4 * groups, LANES), f32),
         pltpu.VMEM((6, groups, LANES), f32),
         pltpu.VMEM((8 * groups, LANES), f32),
         pltpu.VMEM((4, side_groups, LANES), f32),
@@ -359,29 +369,34 @@
         pltpu.VMEM((4, halo, width), f32),
         pltpu.VMEM((6 * groups, LANES), f32),
     ]
+    scratch += [pltpu.VMEM((blocks, size, width), f32) for _, size in CHUNKS]
     for leading in (extended, extended, blocks, 4 * halo, 4 * halo):
         scratch += [pltpu.VMEM((leading, size, width), bf16) for _, size in CHUNKS]
     scratch += [
-        pltpu.SemaphoreType.DMA((12,)),
-        pltpu.SemaphoreType.DMA((len(CHUNKS) + 1,)),
+        pltpu.SemaphoreType.DMA((13 + len(CHUNKS),)),
         pltpu.SemaphoreType.DMA((slots, 4)),
         pltpu.SemaphoreType.DMA((slots, 4)),
     ]
-    traces, modes = pl.pallas_call(
+    shapes = ((blocks, rows, width), (4 * groups, LANES))
+    results = pl.pallas_call(
         functools.partial(kernel, n_wide, n_narrow),
-        out_shape=(
-            jax.ShapeDtypeStruct((blocks, rows, width), f32),
-            jax.ShapeDtypeStruct((4 * groups, LANES), f32),
-        ),
-        in_specs=[pl.BlockSpec(memory_space=pltpu.SMEM)] * 2
-        + [pl.BlockSpec(memory_space=pltpu.HBM)] * 12,
-        out_specs=(pl.BlockSpec(memory_space=pl.ANY),) * 2,
+        out_shape=tuple(pltpu.VMEM(shape, f32) for shape in shapes),
+        in_specs=[pl.BlockSpec(memory_space=pltpu.HBM)] * len(operands),
+        out_specs=(pl.BlockSpec(memory_space=pltpu.VMEM),) * 2,
         scratch_shapes=scratch,
         compiler_params=pltpu.CompilerParams(
-            collective_id=0, has_side_effects=True, vmem_limit_bytes=32 * 1024 * 1024
+            collective_id=0, has_side_effects=True, vmem_limit_bytes=VMEM_LIMIT
         ),
         name="smooth_and_section",
-    )(*operands)
+    )(*(pltpu.with_memory_space_constraint(x, pltpu.HBM) for x in operands))
+    traces, modes = pl.pallas_call(
+        write_back,
+        out_shape=tuple(jax.ShapeDtypeStruct(shape, f32) for shape in shapes),
+        in_specs=[pl.BlockSpec(memory_space=pl.ANY)] * 2,
+        out_specs=(pl.BlockSpec(memory_space=pl.ANY),) * 2,
+        scratch_shapes=[pltpu.SemaphoreType.DMA((2,))],
+        name="write_back",
+    )(*(pltpu.with_memory_space_constraint(x, pltpu.VMEM) for x in results))
     modes = modes.reshape(groups, 4, LANES).transpose(1, 0, 2).reshape(1, 1, 4, cells)
     return traces[None, None], modes
 

time: 33.6 us -> 21.6 us (0.64); the launches traced: 33 us -> 21.5 us
  local copies, waits for them, and re-layouts: 11 us -> 0 us
  Pallas kernels: 21.3 us -> 20.8 us
    unnamed x30 -> x0, local copies, waits for them, and re-layouts: 11 us -> none
    pallas_call x1 -> x2, Pallas kernels: 21.3 us -> 20.8 us  [the longest x1 19.8 us: per_device(): pl.pallas_call(functools.partial(kernel, n_wide, n_narrow), out_shape=tup...]
where the time goes in v2:
time: 21.6 us; the launch traced here: 21.5 us
  Pallas kernels  20.8 us (96%)
  between operations  0.64 us (3%)
    pallas_call x1, Pallas kernels, per_device(): pl.pallas_call(functools.partial(kernel, n_wide, n_narrow), out_shape=tup...  19.8 us
    pallas_call x1, Pallas kernels, per_device(): pl.pallas_call(write_back, out_shape=tuple((jax.ShapeDtypeStruct(shape, f...  0.99 us

profile of v2, /device:TPU:386, one launch (start us, length us, event | category | flops | bytes accessed | tf_op | source)
XLA Modules:
  0.0 21.5 jit_solution(2124017836364667366)
XLA Ops:
  0.6 19.8 %smooth_and_section.1 = (f32[16,128,128]{2,1,0:T(8,128)S(1)}, f32[64,128]{1,0:T(8,128)S(1)}) custom-call(s32[2,16]{1,0:T(2,128)} %bitcast.44, s32[2,4]{1,0:T(2,128)} %bitcast.45, f32[16,128,128]{2,1,0:T(8,128)} %bitcast.32, f32[16,128,128]{2,1,0:T(8,128)} %bitcast.33, bf16[16,128,128]{2,1,0:T(8,128)(2,1)} %bitcast.35, bf16[16,2,128,128]{3,2,1,0:T(8,128)(2,1)} %bitcast.34, ...), custom_call_target="tpu_custom_call" | custom-call | tf_op jit(solution)/shard_map/smooth_and_section/pallas_call | solution.py:381
  20.5 1.0 %write_back.1 = (f32[16,128,128]{2,1,0:T(8,128)}, f32[64,128]{1,0:T(8,128)}) custom-call(f32[16,128,128]{2,1,0:T(8,128)S(1)} %get-tuple-element.6.traces, f32[64,128]{1,0:T(8,128)S(1)} %get-tuple-element.7.modes), custom_call_target="tpu_custom_call" | custom-call | tf_op jit(solution)/shard_map/write_back/pallas_call | solution.py:392

commit v3 on v2

--- a/solution.py
+++ b/solution.py
@@ -19,11 +19,12 @@
     return lax.dot_general(a, b, (((1,), (1,)), ((), ())), preferred_element_type=jnp.float32)
 
 
-def pick_lanes(index, rows):
+def pick_lanes(index, rows, first=0, result=None):
     low = index % LANES
     group = index // LANES
-    result = jnp.zeros(index.shape, jnp.float32)
-    for at, row in enumerate(rows):
+    if result is None:
+        result = jnp.zeros(index.shape, jnp.float32)
+    for at, row in enumerate(rows, first):
         spread = jnp.broadcast_to(row, index.shape)
         taken = jnp.take_along_axis(spread, low, axis=1, mode="promise_in_bounds")
         result = jnp.where(group == at, taken, result)
@@ -76,7 +77,6 @@
     guess, rest = rest[:count], rest[count:]
     first_ext, rest = rest[:count], rest[count:]
     second_ext, rest = rest[:count], rest[count:]
-    second_own, rest = rest[:count], rest[count:]
     first_out, rest = rest[:count], rest[count:]
     second_out, rest = rest[:count], rest[count:]
     load_sem, send_sem, recv_sem = rest
@@ -88,13 +88,6 @@
     there = (i > 0, i < n_wide - 1, j > 0, j < n_narrow - 1)
     device = ((i - 1, j), (i + 1, j), (i, j - 1), (i, j + 1))
 
-    barrier = pltpu.get_barrier_semaphore()
-    for side in range(4):
-
-        @pl.when(there[side])
-        def _():
-            pl.semaphore_signal(barrier, inc=1, device_id=device[side], device_id_type=MESH)
-
     def load(at, src, dst):
         copy = pltpu.make_async_copy(src, dst, load_sem.at[at])
         copy.start()
@@ -104,27 +97,13 @@
     load_guess = []
     for part, (low, size) in enumerate(CHUNKS):
         load_guess.append(load(1 + part, guess_hbm.at[:, pl.ds(low, size)], guess[part]))
-    load_links = load(1 + count, links_hbm, links)
-    loads = [
-        load(2 + count + at, src, dst)
-        for at, (src, dst) in enumerate(
-            (
-                (modes_hbm, modes),
-                (outbound_hbm, outbound),
-                (couple_hbm, couple),
-                (rhs_hbm, rhs),
-                (inverse_hbm, inverse),
-                (near_hbm, near),
-                (flags_hbm, flags),
-                (faces_hbm, faces),
-                (coeff_hbm, coeff),
-                (source_hbm, source),
-                (ratio_hbm, ratio),
-            )
-        )
-    ]
-    load_modes, load_outbound, load_couple, load_rhs, load_inverse, load_near, load_flags = loads[:7]
-    load_cells = loads[7:]
+
+    barrier = pltpu.get_barrier_semaphore()
+    for side in range(4):
+
+        @pl.when(there[side])
+        def _():
+            pl.semaphore_signal(barrier, inc=1, device_id=device[side], device_id_type=MESH)
 
     def remote(src, dst, slot, side):
         return pltpu.make_async_remote_copy(
@@ -190,6 +169,28 @@
         if part == 0:
             pl.semaphore_wait(barrier, sum(x.astype(jnp.int32) for x in there))
         start(part, *block_refs(first_out[part], first_ext[part]))
+        if part == 0:
+            load_links = load(1 + count, links_hbm, links)
+            loads = [
+                load(2 + count + at, src, dst)
+                for at, (src, dst) in enumerate(
+                    (
+                        (couple_hbm, couple),
+                        (inverse_hbm, inverse),
+                        (rhs_hbm, rhs),
+                        (modes_hbm, modes),
+                        (outbound_hbm, outbound),
+                        (near_hbm, near),
+                        (flags_hbm, flags),
+                        (faces_hbm, faces),
+                        (coeff_hbm, coeff),
+                        (source_hbm, source),
+                        (ratio_hbm, ratio),
+                    )
+                )
+            ]
+    load_couple, load_inverse, load_rhs, load_modes, load_outbound, load_near, load_flags = loads[:7]
+    load_cells = loads[7:]
 
     cell_slot, face_slot = 2 * count, 2 * count + 1
     load_modes.wait()
@@ -221,6 +222,35 @@
         for b in range(blocks):
             first_ext[part][b] = guess[part][b].astype(jnp.bfloat16)
 
+    def smooth(extended, low, size, b):
+        pair = jnp.concatenate([extended[links[0, b]], extended[links[1, b]]], axis=1)
+        weight = jnp.concatenate([couple[b, 0], couple[b, 1]], axis=1)
+        coupled = nt_dot(pair, weight)
+        resid = (rhs[b, low : low + size, :] - coupled).astype(jnp.bfloat16)
+        return nt_dot(resid, inverse[b])
+
+    load_links.wait()
+    load_couple.wait()
+    load_rhs.wait()
+    load_inverse.wait()
+
+    def listed(extended, low, size, out):
+        for side in range(4):
+            for h in range(halo):
+                out(side, h, smooth(extended, low, size, sends[h, side]))
+
+    for part, (low, size) in enumerate(CHUNKS):
+
+        def keep(side, h, new):
+            second_out[part][side * halo + h] = new.astype(jnp.bfloat16)
+
+        wait_arrived(part, *block_refs(first_out[part], first_ext[part]))
+        listed(first_ext[part], low, size, keep)
+        start(count + part, *block_refs(second_out[part], second_ext[part]))
+    for part, (low, size) in enumerate(CHUNKS):
+        for b in range(blocks):
+            second_ext[part][b] = smooth(first_ext[part], low, size, b).astype(jnp.bfloat16)
+
     load_near.wait()
     load_flags.wait()
     wait_arrived(cell_slot, *cell_refs)
@@ -235,48 +265,28 @@
         across = pick_lanes(index, rows)
         upwind[at, :] = jnp.where(flags[at, :] == 1, own, across)
 
-    def smooth(extended, low, size, b):
-        pair = jnp.concatenate([extended[links[0, b]], extended[links[1, b]]], axis=1)
-        weight = jnp.concatenate([couple[b, 0], couple[b, 1]], axis=1)
-        coupled = nt_dot(pair, weight)
-        resid = (rhs[b, low : low + size, :] - coupled).astype(jnp.bfloat16)
-        return nt_dot(resid, inverse[b])
-
-    load_links.wait()
-    load_couple.wait()
-    load_rhs.wait()
-    load_inverse.wait()
-    for part, (low, size) in enumerate(CHUNKS):
-        wait_arrived(part, *block_refs(first_out[part], first_ext[part]))
-        for b in range(blocks):
-            new = smooth(first_ext[part], low, size, b).astype(jnp.bfloat16)
-            second_own[part][b] = new
-            second_ext[part][b] = new
-        for side in range(4):
-            for h in range(halo):
-                second_out[part][side * halo + h] = second_own[part][sends[h, side]]
-        start(count + part, *block_refs(second_out[part], second_ext[part]))
+    def keep_row(side, h, new):
+        face_out[side, h : h + 1, :] = new[0:1, :].astype(jnp.bfloat16).astype(jnp.float32)
 
     face_refs = (lambda side: face_out.at[side], lambda side: face_in.at[side])
     for part, (low, size) in enumerate(CHUNKS):
         wait_arrived(count + part, *block_refs(second_out[part], second_ext[part]))
+        if part == 0:
+            listed(second_ext[part], low, size, keep_row)
+            start(face_slot, *face_refs)
         for b in range(blocks):
             new = smooth(second_ext[part], low, size, b)
             traces[b, low : low + size, :] = new
             if part == 0:
                 face_own[b] = new[0:1, :].astype(jnp.bfloat16).astype(jnp.float32)
-        if part == 0:
-            for side in range(4):
-                for h in range(halo):
-                    face_out[side, h : h + 1, :] = face_own[sends[h, side]]
-            start(face_slot, *face_refs)
 
     for copy in load_cells:
         copy.wait()
+    face_index = faces[...]
+    face_trace = pick_lanes(face_index, [face_own[b] for b in range(blocks)])
     wait_arrived(face_slot, *face_refs)
-    rows = [face_own[b] for b in range(blocks)]
-    rows = rows + [face_in[side, h : h + 1, :] for side in range(4) for h in range(halo)]
-    face_trace = pick_lanes(faces[...], rows)
+    rows = [face_in[side, h : h + 1, :] for side in range(4) for h in range(halo)]
+    face_trace = pick_lanes(face_index, rows, blocks, face_trace)
     weights = [coeff[f * groups : (f + 1) * groups, :] for f in range(6)]
     values = [face_trace[f * groups : (f + 1) * groups, :] for f in range(6)]
     total = sum(weights[1:], weights[0])
@@ -370,7 +380,7 @@
         pltpu.VMEM((6 * groups, LANES), f32),
     ]
     scratch += [pltpu.VMEM((blocks, size, width), f32) for _, size in CHUNKS]
-    for leading in (extended, extended, blocks, 4 * halo, 4 * halo):
+    for leading in (extended, extended, 4 * halo, 4 * halo):
         scratch += [pltpu.VMEM((leading, size, width), bf16) for _, size in CHUNKS]
     scratch += [
         pltpu.SemaphoreType.DMA((13 + len(CHUNKS),)),

time: 21.6 us -> 19.4 us (0.90)
  Pallas kernels: 20.8 us -> 18.5 us
    pallas_call x1, Pallas kernels: 19.8 us -> 17.6 us  [per_device(): pl.pallas_call(functools.partial(kernel, n_wide, n_narrow), out_shape=tup...]
where the time goes in v3:
time: 19.4 us; the launch traced here: 19.2 us
  Pallas kernels  18.5 us (95%)
  between operations  0.64 us (3%)
    pallas_call x1, Pallas kernels, per_device(): pl.pallas_call(functools.partial(kernel, n_wide, n_narrow), out_shape=tup...  17.6 us
    pallas_call x1, Pallas kernels, per_device(): pl.pallas_call(write_back, out_shape=tuple((jax.ShapeDtypeStruct(shape, f...  0.99 us

profile of v3, /device:TPU:386, one launch (start us, length us, event | category | flops | bytes accessed | tf_op | source)
XLA Modules:
  0.0 19.2 jit_solution(4754444374019277170)
XLA Ops:
  0.6 17.6 %smooth_and_section.1 = (f32[16,128,128]{2,1,0:T(8,128)S(1)}, f32[64,128]{1,0:T(8,128)S(1)}) custom-call(s32[2,16]{1,0:T(2,128)} %bitcast.44, s32[2,4]{1,0:T(2,128)} %bitcast.45, f32[16,128,128]{2,1,0:T(8,128)} %bitcast.32, f32[16,128,128]{2,1,0:T(8,128)} %bitcast.33, bf16[16,128,128]{2,1,0:T(8,128)(2,1)} %bitcast.35, bf16[16,2,128,128]{3,2,1,0:T(8,128)(2,1)} %bitcast.34, ...), custom_call_target="tpu_custom_call" | custom-call | tf_op jit(solution)/shard_map/smooth_and_section/pallas_call | solution.py:391
  18.2 1.0 %write_back.1 = (f32[16,128,128]{2,1,0:T(8,128)}, f32[64,128]{1,0:T(8,128)}) custom-call(f32[16,128,128]{2,1,0:T(8,128)S(1)} %get-tuple-element.6.traces, f32[64,128]{1,0:T(8,128)S(1)} %get-tuple-element.7.modes), custom_call_target="tpu_custom_call" | custom-call | tf_op jit(solution)/shard_map/write_back/pallas_call | solution.py:402

commit v4 on v3

--- a/solution.py
+++ b/solution.py
@@ -31,7 +31,7 @@
     return result
 
 
-def kernel(
+def smooth_kernel(
     n_wide,
     n_narrow,
     links_hbm,
@@ -49,20 +49,22 @@
     modes_hbm,
     ratio_hbm,
     traces,
-    modes_next,
+    partial,
+    face_rows,
+    upwind,
+    faces,
+    coeff,
+    source,
+    modes,
+    ratio,
     links,
     sends,
     rhs,
     inverse,
     couple,
-    faces,
-    coeff,
-    source,
     near,
     flags,
     outbound,
-    modes,
-    ratio,
     tables,
     cell_table,
     cell_out,
@@ -70,7 +72,6 @@
     face_own,
     face_out,
     face_in,
-    upwind,
     *rest,
 ):
     count = len(CHUNKS)
@@ -282,11 +283,41 @@
 
     for copy in load_cells:
         copy.wait()
-    face_index = faces[...]
-    face_trace = pick_lanes(face_index, [face_own[b] for b in range(blocks)])
+    partial[...] = pick_lanes(faces[...], [face_own[b] for b in range(blocks)])
     wait_arrived(face_slot, *face_refs)
-    rows = [face_in[side, h : h + 1, :] for side in range(4) for h in range(halo)]
-    face_trace = pick_lanes(face_index, rows, blocks, face_trace)
+    for side in range(4):
+        for h in range(halo):
+            face_rows[side * halo + h : side * halo + h + 1, :] = face_in[side, h : h + 1, :]
+
+    for part in range(count):
+        wait_sent(part, *block_refs(first_out[part], first_ext[part]))
+        wait_sent(count + part, *block_refs(second_out[part], second_ext[part]))
+    wait_sent(cell_slot, *cell_refs)
+    wait_sent(face_slot, *face_refs)
+
+
+def section(
+    blocks,
+    traces,
+    partial,
+    face_rows,
+    upwind,
+    faces,
+    coeff,
+    source,
+    modes,
+    ratio,
+    traces_out,
+    modes_out,
+    modes_next,
+    sem,
+):
+    write_traces = pltpu.make_async_copy(traces, traces_out, sem.at[0])
+    write_traces.start()
+    rows = [face_rows[h : h + 1, :] for h in range(face_rows.shape[0])]
+    face_trace = pick_lanes(faces[...], rows, blocks, partial[...])
+    groups = source.shape[0]
+    mode = [modes[pl.ds(m, groups, stride=4), :] for m in range(4)]
     weights = [coeff[f * groups : (f + 1) * groups, :] for f in range(6)]
     values = [face_trace[f * groups : (f + 1) * groups, :] for f in range(6)]
     total = sum(weights[1:], weights[0])
@@ -302,22 +333,10 @@
         modes_next[pl.ds(m, groups, stride=4), :] = mode[m] + 3.0 * step * (
             volume - (flow[hi] - flow[lo])
         )
-    for part in range(count):
-        wait_sent(part, *block_refs(first_out[part], first_ext[part]))
-        wait_sent(count + part, *block_refs(second_out[part], second_ext[part]))
-    wait_sent(cell_slot, *cell_refs)
-    wait_sent(face_slot, *face_refs)
-
-
-def write_back(traces, modes, traces_out, modes_out, sem):
-    copies = [
-        pltpu.make_async_copy(traces, traces_out, sem.at[0]),
-        pltpu.make_async_copy(modes, modes_out, sem.at[1]),
-    ]
-    for copy in copies:
-        copy.start()
-    for copy in copies:
-        copy.wait()
+    write_modes = pltpu.make_async_copy(modes_next, modes_out, sem.at[1])
+    write_modes.start()
+    write_traces.wait()
+    write_modes.wait()
 
 
 def per_device(
@@ -368,7 +387,7 @@
     extended = blocks + 4 * halo
     slots = 2 * len(CHUNKS) + 2
     scratch = [pltpu.SMEM(x.shape, x.dtype) for x in operands[:2]]
-    scratch += [pltpu.VMEM(x.shape, x.dtype) for x in operands[3:]]
+    scratch += [pltpu.VMEM(operands[at].shape, operands[at].dtype) for at in (3, 4, 5, 9, 10, 11)]
     scratch += [
         pltpu.VMEM((6, groups, LANES), f32),
         pltpu.VMEM((8 * groups, LANES), f32),
@@ -377,7 +396,6 @@
         pltpu.VMEM((blocks, 1, width), f32),
         pltpu.VMEM((4, halo, width), f32),
         pltpu.VMEM((4, halo, width), f32),
-        pltpu.VMEM((6 * groups, LANES), f32),
     ]
     scratch += [pltpu.VMEM((blocks, size, width), f32) for _, size in CHUNKS]
     for leading in (extended, extended, 4 * halo, 4 * halo):
@@ -387,25 +405,31 @@
         pltpu.SemaphoreType.DMA((slots, 4)),
         pltpu.SemaphoreType.DMA((slots, 4)),
     ]
-    shapes = ((blocks, rows, width), (4 * groups, LANES))
+    cells_shape = (6 * groups, LANES)
+    shapes = [(blocks, rows, width), cells_shape, (4 * halo, width), cells_shape]
+    kept = [(shape, f32) for shape in shapes]
+    kept += [(operands[at].shape, operands[at].dtype) for at in (6, 7, 8, 12, 13)]
     results = pl.pallas_call(
-        functools.partial(kernel, n_wide, n_narrow),
-        out_shape=tuple(pltpu.VMEM(shape, f32) for shape in shapes),
+        functools.partial(smooth_kernel, n_wide, n_narrow),
+        out_shape=tuple(pltpu.VMEM(*x) for x in kept),
         in_specs=[pl.BlockSpec(memory_space=pltpu.HBM)] * len(operands),
-        out_specs=(pl.BlockSpec(memory_space=pltpu.VMEM),) * 2,
+        out_specs=(pl.BlockSpec(memory_space=pltpu.VMEM),) * len(kept),
         scratch_shapes=scratch,
         compiler_params=pltpu.CompilerParams(
             collective_id=0, has_side_effects=True, vmem_limit_bytes=VMEM_LIMIT
         ),
-        name="smooth_and_section",
+        name="smooth",
     )(*(pltpu.with_memory_space_constraint(x, pltpu.HBM) for x in operands))
     traces, modes = pl.pallas_call(
-        write_back,
-        out_shape=tuple(jax.ShapeDtypeStruct(shape, f32) for shape in shapes),
-        in_specs=[pl.BlockSpec(memory_space=pl.ANY)] * 2,
+        functools.partial(section, blocks),
+        out_shape=(
+            jax.ShapeDtypeStruct(shapes[0], f32),
+            jax.ShapeDtypeStruct((4 * groups, LANES), f32),
+        ),
+        in_specs=[pl.BlockSpec(memory_space=pltpu.VMEM)] * len(kept),
         out_specs=(pl.BlockSpec(memory_space=pl.ANY),) * 2,
-        scratch_shapes=[pltpu.SemaphoreType.DMA((2,))],
-        name="write_back",
+        scratch_shapes=[pltpu.VMEM((4 * groups, LANES), f32), pltpu.SemaphoreType.DMA((2,))],
+        name="section",
     )(*(pltpu.with_memory_space_constraint(x, pltpu.VMEM) for x in results))
     modes = modes.reshape(groups, 4, LANES).transpose(1, 0, 2).reshape(1, 1, 4, cells)
     return traces[None, None], modes

time: 19.4 us -> 19 us (0.979)
  Pallas kernels: 18.5 us -> 18.2 us
    pallas_call x2, Pallas kernels: 18.5 us -> 18.2 us  [the longest x1 17.2 us: per_device(): pl.pallas_call(functools.partial(smooth_kernel, n_wide, n_narrow), out_sh...]
where the time goes in v4:
time: 19 us; the launch traced here: 18.9 us
  Pallas kernels  18.2 us (96%)
  between operations  0.64 us (3%)
    pallas_call x1, Pallas kernels, per_device(): pl.pallas_call(functools.partial(smooth_kernel, n_wide, n_narrow), out_sh...  17.2 us
    pallas_call x1, Pallas kernels, per_device(): pl.pallas_call(functools.partial(section, blocks), out_shape=(jax.ShapeDt...  0.99 us

profile of v4, /device:TPU:386, one launch (start us, length us, event | category | flops | bytes accessed | tf_op | source)
XLA Modules:
  0.0 18.9 jit_solution(12653557458200087000)
XLA Ops:
  0.6 17.2 %smooth.1 = (f32[16,128,128]{2,1,0:T(8,128)S(1)}, f32[96,128]{1,0:T(8,128)S(1)}, f32[8,128]{1,0:T(8,128)S(1)}, f32[96,128]{1,0:T(8,128)S(1)}, s32[96,128]{1,0:T(...) custom-call(s32[2,16]{1,0:T(2,128)} %bitcast.44, ...), custom_call_target="tpu_custom_call" | custom-call | tf_op jit(solution)/shard_map/smooth/pallas_call | solution.py:412
  17.9 1.0 %section.1 = (f32[16,128,128]{2,1,0:T(8,128)}, f32[64,128]{1,0:T(8,128)}) custom-call(f32[16,128,128]{2,1,0:T(8,128)S(1)} %get-tuple-element.13.traces, f32[96,128]{1,0:T(8,128)S(1)} %get-tuple-element.14.partial, f32[8,128]{1,0:T(8,128)S(1)} %get-tuple-element.15.face_rows, f32[96,128]{1,0:T(8,128)S(1)} %get-tuple-element.16.upwind, ...), custom_call_target="tpu_custom_call" | custom-call | tf_op jit(solution)/shard_map/section/pallas_call | solution.py:423

commit v5 on v4

--- a/solution.py
+++ b/solution.py
@@ -223,22 +223,30 @@
         for b in range(blocks):
             first_ext[part][b] = guess[part][b].astype(jnp.bfloat16)
 
-    def smooth(extended, low, size, b):
-        pair = jnp.concatenate([extended[links[0, b]], extended[links[1, b]]], axis=1)
+    def residual(extended, low, size, b, one, two):
+        pair = jnp.concatenate([extended[one], extended[two]], axis=1)
         weight = jnp.concatenate([couple[b, 0], couple[b, 1]], axis=1)
         coupled = nt_dot(pair, weight)
-        resid = (rhs[b, low : low + size, :] - coupled).astype(jnp.bfloat16)
-        return nt_dot(resid, inverse[b])
+        return (rhs[b, low : low + size, :] - coupled).astype(jnp.bfloat16)
+
+    def smooth(extended, low, size, b):
+        return nt_dot(residual(extended, low, size, b, links[0, b], links[1, b]), inverse[b])
 
     load_links.wait()
     load_couple.wait()
     load_rhs.wait()
     load_inverse.wait()
 
+    spots = [(side, h) for side in range(4) for h in range(halo)]
+    spot_blocks = []
+    for side, h in spots:
+        b = sends[h, side]
+        spot_blocks.append((b, links[0, b], links[1, b]))
+
     def listed(extended, low, size, out):
-        for side in range(4):
-            for h in range(halo):
-                out(side, h, smooth(extended, low, size, sends[h, side]))
+        resids = [residual(extended, low, size, *at) for at in spot_blocks]
+        for (side, h), resid, at in zip(spots, resids, spot_blocks):
+            out(side, h, nt_dot(resid, inverse[at[0]]))
 
     for part, (low, size) in enumerate(CHUNKS):
 

time: 19 us -> 18.8 us (0.989)
  Pallas kernels: 18.2 us -> 18 us
    pallas_call x1, Pallas kernels: 17.2 us -> 17 us  [per_device(): pl.pallas_call(functools.partial(smooth_kernel, n_wide, n_narrow), out_sh...]
where the time goes in v5:
time: 18.8 us; the launch traced here: 18.6 us
  Pallas kernels  18 us (96%)
  between operations  0.64 us (3%)
    pallas_call x1, Pallas kernels, per_device(): pl.pallas_call(functools.partial(smooth_kernel, n_wide, n_narrow), out_sh...  17 us
    pallas_call x1, Pallas kernels, per_device(): pl.pallas_call(functools.partial(section, blocks), out_shape=(jax.ShapeDt...  0.99 us

profile of v5, /device:TPU:386, one launch (start us, length us, event | category | flops | bytes accessed | tf_op | source)
XLA Modules:
  0.0 18.6 jit_solution(5256724253259072649)
XLA Ops:
  0.6 17.0 %smooth.1 = (f32[16,128,128]{2,1,0:T(8,128)S(1)}, f32[96,128]{1,0:T(8,128)S(1)}, f32[8,128]{1,0:T(8,128)S(1)}, f32[96,128]{1,0:T(8,128)S(1)}, s32[96,128]{1,0:T(...) custom-call(s32[2,16]{1,0:T(2,128)} %bitcast.44, ...), custom_call_target="tpu_custom_call" | custom-call | tf_op jit(solution)/shard_map/smooth/pallas_call | solution.py:420
  17.6 1.0 %section.1 = (f32[16,128,128]{2,1,0:T(8,128)}, f32[64,128]{1,0:T(8,128)}) custom-call(f32[16,128,128]{2,1,0:T(8,128)S(1)} %get-tuple-element.13.traces, f32[96,128]{1,0:T(8,128)S(1)} %get-tuple-element.14.partial, f32[8,128]{1,0:T(8,128)S(1)} %get-tuple-element.15.face_rows, f32[96,128]{1,0:T(8,128)S(1)} %get-tuple-element.16.upwind, ...), custom_call_target="tpu_custom_call" | custom-call | tf_op jit(solution)/shard_map/section/pallas_call | solution.py:431

commit v6 on v5

--- a/solution.py
+++ b/solution.py
@@ -10,7 +10,7 @@
 MESH = pl.DeviceIdType.MESH
 LANES = 128
 VMEM_LIMIT = 48 * 1024 * 1024
-CHUNKS = ((0, 16), (16, 112))
+TOP = 8
 
 OPPOSITE = (1, 0, 3, 2)
 
@@ -74,12 +74,8 @@
     face_in,
     *rest,
 ):
-    count = len(CHUNKS)
-    guess, rest = rest[:count], rest[count:]
-    first_ext, rest = rest[:count], rest[count:]
-    second_ext, rest = rest[:count], rest[count:]
-    first_out, rest = rest[:count], rest[count:]
-    second_out, rest = rest[:count], rest[count:]
+    top_guess, top_first, top_second, top_first_out, top_second_out, rest = *rest[:5], rest[5:]
+    guess, first_ext, second_ext, first_out, second_out, rest = *rest[:5], rest[5:]
     load_sem, send_sem, recv_sem = rest
     blocks = rhs.shape[0]
     halo = sends.shape[0]
@@ -95,9 +91,8 @@
         return copy
 
     load_sends = load(0, sends_hbm, sends)
-    load_guess = []
-    for part, (low, size) in enumerate(CHUNKS):
-        load_guess.append(load(1 + part, guess_hbm.at[:, pl.ds(low, size)], guess[part]))
+    load_top = load(1, guess_hbm.at[:, pl.ds(0, TOP)], top_guess)
+    load_guess = load(2, guess_hbm, guess)
 
     barrier = pltpu.get_barrier_semaphore()
     for side in range(4):
@@ -143,57 +138,58 @@
             lambda side: extended.at[pl.ds(blocks + side * halo, halo)],
         )
 
-    for part in range(count):
-        for side in range(4):
-
-            @pl.when(jnp.logical_not(there[side]))
-            def _():
-                at = pl.ds(blocks + side * halo, halo)
-                empty = jnp.zeros((halo,) + first_ext[part].shape[1:], jnp.bfloat16)
-                first_ext[part][at] = empty
-                second_ext[part][at] = empty
-
     for side in range(4):
 
         @pl.when(jnp.logical_not(there[side]))
         def _():
+            at = pl.ds(blocks + side * halo, halo)
+            for extended in (top_first, top_second, first_ext, second_ext):
+                extended[at] = jnp.zeros((halo,) + extended.shape[1:], extended.dtype)
             cell_in[side] = jnp.zeros(cell_in.shape[1:], jnp.float32)
             face_in[side] = jnp.zeros(face_in.shape[1:], jnp.float32)
 
+    def rounded(row):
+        return row.astype(jnp.bfloat16).astype(jnp.float32)
+
+    top_first_refs = block_refs(top_first_out, top_first)
+    top_second_refs = block_refs(top_second_out, top_second)
+    first_refs = block_refs(first_out, first_ext)
+    second_refs = block_refs(second_out, second_ext)
+    spots = [(side, h) for side in range(4) for h in range(halo)]
+
     load_sends.wait()
-    for part, (low, size) in enumerate(CHUNKS):
-        load_guess[part].wait()
-        for side in range(4):
-            for h in range(halo):
-                picked = guess[part][sends[h, side]]
-                first_out[part][side * halo + h] = picked.astype(jnp.bfloat16)
-        if part == 0:
-            pl.semaphore_wait(barrier, sum(x.astype(jnp.int32) for x in there))
-        start(part, *block_refs(first_out[part], first_ext[part]))
-        if part == 0:
-            load_links = load(1 + count, links_hbm, links)
-            loads = [
-                load(2 + count + at, src, dst)
-                for at, (src, dst) in enumerate(
-                    (
-                        (couple_hbm, couple),
-                        (inverse_hbm, inverse),
-                        (rhs_hbm, rhs),
-                        (modes_hbm, modes),
-                        (outbound_hbm, outbound),
-                        (near_hbm, near),
-                        (flags_hbm, flags),
-                        (faces_hbm, faces),
-                        (coeff_hbm, coeff),
-                        (source_hbm, source),
-                        (ratio_hbm, ratio),
-                    )
-                )
-            ]
+    load_top.wait()
+    for side, h in spots:
+        top_first_out[side * halo + h] = rounded(top_guess[sends[h, side], 0:1, :])
+    pl.semaphore_wait(barrier, sum(x.astype(jnp.int32) for x in there))
+    start(0, *top_first_refs)
+    load_links = load(3, links_hbm, links)
+    loads = [
+        load(4 + at, src, dst)
+        for at, (src, dst) in enumerate(
+            (
+                (couple_hbm, couple),
+                (inverse_hbm, inverse),
+                (rhs_hbm, rhs),
+                (modes_hbm, modes),
+                (outbound_hbm, outbound),
+                (near_hbm, near),
+                (flags_hbm, flags),
+                (faces_hbm, faces),
+                (coeff_hbm, coeff),
+                (source_hbm, source),
+                (ratio_hbm, ratio),
+            )
+        )
+    ]
     load_couple, load_inverse, load_rhs, load_modes, load_outbound, load_near, load_flags = loads[:7]
     load_cells = loads[7:]
-
-    cell_slot, face_slot = 2 * count, 2 * count + 1
+    load_guess.wait()
+    for side, h in spots:
+        first_out[side * halo + h] = guess[sends[h, side]].astype(jnp.bfloat16)
+    start(1, *first_refs)
+
+    cell_slot, face_slot = 4, 5
     load_modes.wait()
     load_outbound.wait()
     groups = modes.shape[0] // 4
@@ -219,46 +215,49 @@
     cell_refs = (lambda side: cell_out.at[side], lambda side: cell_in.at[side])
     start(cell_slot, *cell_refs)
 
-    for part, (low, size) in enumerate(CHUNKS):
-        for b in range(blocks):
-            first_ext[part][b] = guess[part][b].astype(jnp.bfloat16)
-
-    def residual(extended, low, size, b, one, two):
-        pair = jnp.concatenate([extended[one], extended[two]], axis=1)
-        weight = jnp.concatenate([couple[b, 0], couple[b, 1]], axis=1)
-        coupled = nt_dot(pair, weight)
-        return (rhs[b, low : low + size, :] - coupled).astype(jnp.bfloat16)
-
-    def smooth(extended, low, size, b):
-        return nt_dot(residual(extended, low, size, b, links[0, b], links[1, b]), inverse[b])
+    for b in range(blocks):
+        top_first[b] = rounded(top_guess[b, 0:1, :])
+        first_ext[b] = guess[b].astype(jnp.bfloat16)
 
     load_links.wait()
     load_couple.wait()
     load_rhs.wait()
     load_inverse.wait()
-
-    spots = [(side, h) for side in range(4) for h in range(halo)]
     spot_blocks = []
     for side, h in spots:
         b = sends[h, side]
         spot_blocks.append((b, links[0, b], links[1, b]))
 
-    def listed(extended, low, size, out):
-        resids = [residual(extended, low, size, *at) for at in spot_blocks]
-        for (side, h), resid, at in zip(spots, resids, spot_blocks):
-            out(side, h, nt_dot(resid, inverse[at[0]]))
-
-    for part, (low, size) in enumerate(CHUNKS):
-
-        def keep(side, h, new):
-            second_out[part][side * halo + h] = new.astype(jnp.bfloat16)
-
-        wait_arrived(part, *block_refs(first_out[part], first_ext[part]))
-        listed(first_ext[part], low, size, keep)
-        start(count + part, *block_refs(second_out[part], second_ext[part]))
-    for part, (low, size) in enumerate(CHUNKS):
-        for b in range(blocks):
-            second_ext[part][b] = smooth(first_ext[part], low, size, b).astype(jnp.bfloat16)
+    def residual(extended, b, one, two):
+        pair = jnp.concatenate([extended[one], extended[two]], axis=1).astype(jnp.bfloat16)
+        weight = jnp.concatenate([couple[b, 0], couple[b, 1]], axis=1)
+        return (rhs[b, 0 : pair.shape[0], :] - nt_dot(pair, weight)).astype(jnp.bfloat16)
+
+    def listed(extended):
+        resids = [residual(extended, *at) for at in spot_blocks]
+        return [nt_dot(resid, inverse[at[0]]) for resid, at in zip(resids, spot_blocks)]
+
+    def smooth(extended, b):
+        return nt_dot(residual(extended, b, links[0, b], links[1, b]), inverse[b])
+
+    wait_arrived(0, *top_first_refs)
+    for (side, h), new in zip(spots, listed(top_first)):
+        top_second_out[side * halo + h] = rounded(new)
+    start(2, *top_second_refs)
+    wait_arrived(1, *first_refs)
+    for (side, h), new in zip(spots, listed(first_ext)):
+        second_out[side * halo + h] = new.astype(jnp.bfloat16)
+    start(3, *second_refs)
+    for b in range(blocks):
+        new = smooth(first_ext, b)
+        top_second[b] = rounded(new[0:1, :])
+        second_ext[b] = new.astype(jnp.bfloat16)
+
+    face_refs = (lambda side: face_out.at[side], lambda side: face_in.at[side])
+    wait_arrived(2, *top_second_refs)
+    for (side, h), new in zip(spots, listed(top_second)):
+        face_out[side, h : h + 1, :] = rounded(new)
+    start(face_slot, *face_refs)
 
     load_near.wait()
     load_flags.wait()
@@ -274,20 +273,11 @@
         across = pick_lanes(index, rows)
         upwind[at, :] = jnp.where(flags[at, :] == 1, own, across)
 
-    def keep_row(side, h, new):
-        face_out[side, h : h + 1, :] = new[0:1, :].astype(jnp.bfloat16).astype(jnp.float32)
-
-    face_refs = (lambda side: face_out.at[side], lambda side: face_in.at[side])
-    for part, (low, size) in enumerate(CHUNKS):
-        wait_arrived(count + part, *block_refs(second_out[part], second_ext[part]))
-        if part == 0:
-            listed(second_ext[part], low, size, keep_row)
-            start(face_slot, *face_refs)
-        for b in range(blocks):
-            new = smooth(second_ext[part], low, size, b)
-            traces[b, low : low + size, :] = new
-            if part == 0:
-                face_own[b] = new[0:1, :].astype(jnp.bfloat16).astype(jnp.float32)
+    wait_arrived(3, *second_refs)
+    for b in range(blocks):
+        new = smooth(second_ext, b)
+        traces[b] = new
+        face_own[b] = rounded(new[0:1, :])
 
     for copy in load_cells:
         copy.wait()
@@ -297,9 +287,8 @@
         for h in range(halo):
             face_rows[side * halo + h : side * halo + h + 1, :] = face_in[side, h : h + 1, :]
 
-    for part in range(count):
-        wait_sent(part, *block_refs(first_out[part], first_ext[part]))
-        wait_sent(count + part, *block_refs(second_out[part], second_ext[part]))
+    for slot, refs in enumerate((top_first_refs, first_refs, top_second_refs, second_refs)):
+        wait_sent(slot, *refs)
     wait_sent(cell_slot, *cell_refs)
     wait_sent(face_slot, *face_refs)
 
@@ -393,7 +382,6 @@
     )
     f32, bf16 = jnp.float32, jnp.bfloat16
     extended = blocks + 4 * halo
-    slots = 2 * len(CHUNKS) + 2
     scratch = [pltpu.SMEM(x.shape, x.dtype) for x in operands[:2]]
     scratch += [pltpu.VMEM(operands[at].shape, operands[at].dtype) for at in (3, 4, 5, 9, 10, 11)]
     scratch += [
@@ -405,13 +393,15 @@
         pltpu.VMEM((4, halo, width), f32),
         pltpu.VMEM((4, halo, width), f32),
     ]
-    scratch += [pltpu.VMEM((blocks, size, width), f32) for _, size in CHUNKS]
-    for leading in (extended, extended, 4 * halo, 4 * halo):
-        scratch += [pltpu.VMEM((leading, size, width), bf16) for _, size in CHUNKS]
+    scratch += [pltpu.VMEM((blocks, TOP, width), f32)]
+    leadings = (extended, extended, 4 * halo, 4 * halo)
+    scratch += [pltpu.VMEM((leading, 1, width), f32) for leading in leadings]
+    scratch += [pltpu.VMEM((blocks, rows, width), f32)]
+    scratch += [pltpu.VMEM((leading, rows, width), bf16) for leading in leadings]
     scratch += [
-        pltpu.SemaphoreType.DMA((13 + len(CHUNKS),)),
-        pltpu.SemaphoreType.DMA((slots, 4)),
-        pltpu.SemaphoreType.DMA((slots, 4)),
+        pltpu.SemaphoreType.DMA((15,)),
+        pltpu.SemaphoreType.DMA((6, 4)),
+        pltpu.SemaphoreType.DMA((6, 4)),
     ]
     cells_shape = (6 * groups, LANES)
     shapes = [(blocks, rows, width), cells_shape, (4 * halo, width), cells_shape]

time: 18.8 us -> 18.6 us (0.989)
  Pallas kernels: 18 us -> 17.8 us
where the time goes in v6:
time: 18.6 us; the launch traced here: 18.5 us
  Pallas kernels  17.8 us (96%)
  between operations  0.64 us (3%)
    pallas_call x1, Pallas kernels, per_device(): pl.pallas_call(functools.partial(smooth_kernel, n_wide, n_narrow), out_sh...  16.8 us
    pallas_call x1, Pallas kernels, per_device(): pl.pallas_call(functools.partial(section, blocks), out_shape=(jax.ShapeDt...  0.99 us

profile of v6, /device:TPU:386, one launch (start us, length us, event | category | flops | bytes accessed | tf_op | source)
XLA Modules:
  0.0 18.5 jit_solution(12374166140002518624)
XLA Ops:
  0.6 16.8 %smooth.1 = (f32[16,128,128]{2,1,0:T(8,128)S(1)}, f32[96,128]{1,0:T(8,128)S(1)}, f32[8,128]{1,0:T(8,128)S(1)}, f32[96,128]{1,0:T(8,128)S(1)}, s32[96,128]{1,0:T(...) custom-call(s32[2,16]{1,0:T(2,128)} %bitcast.44, ...), custom_call_target="tpu_custom_call" | custom-call | tf_op jit(solution)/shard_map/smooth/pallas_call | solution.py:410
  17.5 1.0 %section.1 = (f32[16,128,128]{2,1,0:T(8,128)}, f32[64,128]{1,0:T(8,128)}) custom-call(f32[16,128,128]{2,1,0:T(8,128)S(1)} %get-tuple-element.13.traces, f32[96,128]{1,0:T(8,128)S(1)} %get-tuple-element.14.partial, f32[8,128]{1,0:T(8,128)S(1)} %get-tuple-element.15.face_rows, f32[96,128]{1,0:T(8,128)S(1)} %get-tuple-element.16.upwind, ...), custom_call_target="tpu_custom_call" | custom-call | tf_op jit(solution)/shard_map/section/pallas_call | solution.py:421

commit v7 on v6

--- a/solution.py
+++ b/solution.py
@@ -273,15 +273,15 @@
         across = pick_lanes(index, rows)
         upwind[at, :] = jnp.where(flags[at, :] == 1, own, across)
 
-    wait_arrived(3, *second_refs)
     for b in range(blocks):
-        new = smooth(second_ext, b)
-        traces[b] = new
-        face_own[b] = rounded(new[0:1, :])
-
+        face_own[b] = rounded(smooth(top_second, b))
     for copy in load_cells:
         copy.wait()
     partial[...] = pick_lanes(faces[...], [face_own[b] for b in range(blocks)])
+
+    wait_arrived(3, *second_refs)
+    for b in range(blocks):
+        traces[b] = smooth(second_ext, b)
     wait_arrived(face_slot, *face_refs)
     for side in range(4):
         for h in range(halo):

time: 18.6 us -> 18.6 us (level)
  no operation moved by 1% of the time
where the time goes in v7:
time: 18.6 us; the launch traced here: 18.5 us
  Pallas kernels  17.8 us (96%)
  between operations  0.64 us (3%)
    pallas_call x1, Pallas kernels, per_device(): pl.pallas_call(functools.partial(smooth_kernel, n_wide, n_narrow), out_sh...  16.8 us
    pallas_call x1, Pallas kernels, per_device(): pl.pallas_call(functools.partial(section, blocks), out_shape=(jax.ShapeDt...  0.99 us

profile of v7, /device:TPU:386, one launch (start us, length us, event | category | flops | bytes accessed | tf_op | source)
XLA Modules:
  0.0 18.5 jit_solution(254310519687203180)
XLA Ops:
  0.6 16.8 %smooth.1 = (f32[16,128,128]{2,1,0:T(8,128)S(1)}, f32[96,128]{1,0:T(8,128)S(1)}, f32[8,128]{1,0:T(8,128)S(1)}, f32[96,128]{1,0:T(8,128)S(1)}, s32[96,128]{1,0:T(...) custom-call(s32[2,16]{1,0:T(2,128)} %bitcast.44, ...), custom_call_target="tpu_custom_call" | custom-call | tf_op jit(solution)/shard_map/smooth/pallas_call | solution.py:410
  17.5 1.0 %section.1 = (f32[16,128,128]{2,1,0:T(8,128)}, f32[64,128]{1,0:T(8,128)}) custom-call(f32[16,128,128]{2,1,0:T(8,128)S(1)} %get-tuple-element.13.traces, f32[96,128]{1,0:T(8,128)S(1)} %get-tuple-element.14.partial, f32[8,128]{1,0:T(8,128)S(1)} %get-tuple-element.15.face_rows, f32[96,128]{1,0:T(8,128)S(1)} %get-tuple-element.16.upwind, ...), custom_call_target="tpu_custom_call" | custom-call | tf_op jit(solution)/shard_map/section/pallas_call | solution.py:421
